TPU v7x, 32 devices: a whole 2x2x4 slice. The times are simulated.
32 devices in a mesh: grp: 2 (over core), aux: 8 (over z, x), tr: 2 (over y).
Axes of the slice: x: 2, y: 2, z: 4, core: 2. Of those that a mesh axis runs over, the one named last changes fastest.
Arguments:
- trial_vectors: float32 [64, 8, 512], P('aux', None, 'tr'), may hold values from -6 to 6
- energy_val: float32 [64], P('aux'), may hold values from -1 to -0.2
- energy_cond: float32 [512], P('tr'), may hold values from 0.2 to 2
- coef_occ: bfloat16 [512, 64, 64], P('aux'), may hold values from -0.75 to 0.75
- coef_virt: bfloat16 [512, 512, 512], P('aux', 'tr'), may hold values from -0.01171875 to 0.01171875
- pair_coef: bfloat16 [64, 512, 512], P('aux', 'tr'), may hold values from -0.03125 to 0.03125
- live_aux: int32 [8], P('aux'), may hold values from 16 to 64, as said below
Outputs:
- applied: float32 [64, 8, 512], P('aux', None, 'tr')
- intersection: float32 [8, 8], replicated
Inputs may be any that keep to these rules, and one draw needn't show every extreme that they name: `live_aux`: equals 64 on at least one shard.
All inputs are finite; a program needn't handle non-finite values.
Results may differ from a plain program's by a relative error of at most 0.0048.
Values may be sent and summed in bfloat16 or wider, within the bound.
A program may use at most 64 MiB of HBM per device.

v0:
```python
import functools

import jax
import jax.numpy as jnp
from jax import lax
from jax.experimental import pallas as pl
from jax.experimental.pallas import tpu as pltpu
from jax.sharding import PartitionSpec as P

F32 = jnp.float32
BF16 = jnp.bfloat16
GROUPS = 1
CHUNK = 32
BLEND = 32
MESH = pl.DeviceIdType.MESH


def kernel(
    naux, ntr, groups,
    live_ref, trial_ref, val_ref, cond_ref, occ_hbm, virt_hbm, pair_hbm,
    out_ref, inter_ref,
    occ, virt, pair, blended, acc, wide, mixed, trial_k,
    block_send, block_recv, proj_send, proj_recv, tr_send, tr_recv,
    sum_send, sum_recv, dots_send, dots_recv, core_recv, final_send, final_recv,
    load_sem, block_ssem, block_rsem, proj_ssem, proj_rsem,
    tr_ssem, tr_rsem, sum_ssem, sum_rsem, dots_ssem, dots_rsem, core_ssem, core_rsem,
):
    g = lax.axis_index("grp")
    a = lax.axis_index("aux")
    t = lax.axis_index("tr")
    own_val, vectors, cond = trial_ref.shape
    half = vectors // 2
    size = half // groups
    slots, val, _ = occ.shape
    other_t = lax.rem(t + 1, ntr)
    own_cols = pl.ds(pl.multiple_of(t * cond, cond), cond)
    other_cols = pl.ds(pl.multiple_of(other_t * cond, cond), cond)

    occ_copy = pltpu.make_async_copy(occ_hbm, occ, load_sem.at[0])
    pair_copy = pltpu.make_async_copy(pair_hbm, pair, load_sem.at[1])
    occ_copy.start()
    pair_copy.start()

    virt_copy = pltpu.make_async_copy(virt_hbm, virt, load_sem.at[2])
    virt_copy.start()

    everyone = [(da, dt) for da in range(naux) for dt in range(ntr) if (da, dt) != (0, 0)]

    def peer(da, dt):
        return {"aux": lax.rem(a + da, naux), "tr": lax.rem(t + dt, ntr)}

    barrier = pltpu.get_barrier_semaphore()
    for da, dt in everyone:
        pl.semaphore_signal(barrier, inc=1, device_id=peer(da, dt), device_id_type=MESH)
    pl.semaphore_signal(barrier, inc=1, device_id={"grp": 1 - g}, device_id_type=MESH)

    square = (own_val, own_val)
    diagonal = lax.broadcasted_iota(jnp.int32, square, 0) == lax.broadcasted_iota(jnp.int32, square, 1)
    val_column = jnp.sum(jnp.where(diagonal, val_ref[...], 0.0), axis=1, keepdims=True)
    gap = cond_ref[...] - val_column
    for k in range(vectors):
        trial_k[k] = trial_ref[:, k, :]

    def to_all(it, send, recv, ssem, rsem):
        copies = []
        for da, dt in everyone:
            n = da * ntr + dt
            copies.append(pltpu.make_async_remote_copy(
                src_ref=send.at[it], dst_ref=recv.at[it, n],
                send_sem=ssem.at[it, n], recv_sem=rsem.at[it, n],
                device_id=peer(da, dt), device_id_type=MESH))
        return copies

    def contract(r, cols):
        acc[...] = jnp.zeros_like(acc)

        @pl.loop(0, slots // CHUNK)
        def _(i):
            acc[...] += jnp.dot(
                blended[r, i], virt[pl.ds(i * CHUNK, CHUNK), :, cols].reshape(CHUNK * cond, cond),
                preferred_element_type=F32)

    def apply(it, x):
        for r in range(groups):
            block = jnp.concatenate(x[r * size:(r + 1) * size], axis=1).astype(BF16)
            block_send[it, r] = block
            block_recv[it, r, a] = block
        if it == 0:
            pl.semaphore_wait(barrier, len(everyone) + 1)
        gathers = []
        for r in range(groups):
            gathers.append([])
            for d in range(1, naux):
                copy = pltpu.make_async_remote_copy(
                    src_ref=block_send.at[it, r], dst_ref=block_recv.at[it, r, a],
                    send_sem=block_ssem.at[it, r, d], recv_sem=block_rsem.at[it, r, d],
                    device_id=peer(d, 0), device_id_type=MESH)
                copy.start()
                gathers[r].append(copy)

        if it == 0:
            pair_copy.wait()
        for k in range(half):
            mixed[:, k, :] = x[k]
        proj = jnp.zeros((half, pair.shape[2]), F32)
        for v in range(own_val):
            proj += jnp.dot(mixed[v].astype(BF16), pair[v], preferred_element_type=F32)
        proj_send[it] = proj.astype(BF16)
        projections = to_all(it, proj_send, proj_recv, proj_ssem, proj_rsem)
        for copy in projections:
            copy.start()

        if it == 0:
            occ_copy.wait()
            live = live_ref[...]

            @pl.loop(0, slots)
            def _(p):
                keep = (p < live).astype(F32)
                occ[p] = (occ[p].astype(F32) * keep).astype(BF16)

        tr_copies = []
        for r in range(groups):
            for copy in gathers[r]:
                copy.wait_recv()
            for s in range(naux):
                wide[pl.ds(s * own_val, own_val), :] = block_recv[it, r, s].astype(F32)
            columns = [wide[:, k * cond:(k + 1) * cond].astype(BF16) for k in range(size)]

            @pl.loop(0, slots // BLEND)
            def _(i):
                rows = occ[pl.ds(i * BLEND, BLEND)].reshape(BLEND * val, val)
                for k in range(size):
                    b = jnp.dot(rows, columns[k], preferred_element_type=F32).astype(BF16)
                    for q in range(BLEND):
                        blended[r, i * (BLEND // CHUNK) + q // CHUNK, k * val:(k + 1) * val,
                                (q % CHUNK) * cond:(q % CHUNK + 1) * cond] = b[q * val:(q + 1) * val]

            if it == 0 and r == 0:
                virt_copy.wait()
            copy = pltpu.make_async_remote_copy(
                src_ref=tr_send.at[it, r], dst_ref=tr_recv.at[it, r],
                send_sem=tr_ssem.at[it, r], recv_sem=tr_rsem.at[it, r],
                device_id=peer(0, 1), device_id_type=MESH)
            tr_copies.append(copy)

            @pl.loop(0, 2)
            def _(j):
                start = pl.multiple_of(lax.rem(t + 1 + j, ntr) * cond, cond)
                contract(r, pl.ds(start, cond))

                @pl.when(j == 0)
                def _():
                    tr_send[it, r] = acc[...].astype(BF16)
                    copy.start()

        sums = []
        for r in range(groups):
            tr_copies[r].wait_recv()
            acc[...] += tr_recv[it, r].astype(F32)
            for s in range(naux):
                for k in range(size):
                    row = k * val + s * own_val
                    sum_send[it, r, s, :, k * cond:(k + 1) * cond] = acc[row:row + own_val, :].astype(BF16)
            for d in range(1, naux):
                copy = pltpu.make_async_remote_copy(
                    src_ref=sum_send.at[it, r, lax.rem(a + d, naux)], dst_ref=sum_recv.at[it, r, d],
                    send_sem=sum_ssem.at[it, r, d], recv_sem=sum_rsem.at[it, r, d],
                    device_id=peer(d, 0), device_id_type=MESH)
                copy.start()
                sums.append(copy)

        for copy in projections:
            copy.wait_recv()
        proj = proj_send[it].astype(F32)
        for da, dt in everyone:
            proj += proj_recv[it, da * ntr + dt].astype(F32)
        proj_b = proj.astype(BF16)
        for v in range(own_val):
            mixed[v] = lax.dot_general(
                proj_b, pair[v], (((1,), (1,)), ((), ())), preferred_element_type=F32)
        for copy in sums:
            copy.wait_recv()
        result = []
        for r in range(groups):
            total = sum_send[it, r, a].astype(F32)
            for d in range(1, naux):
                total += sum_recv[it, r, d].astype(F32)
            for k in range(size):
                n = r * size + k
                result.append(gap * x[n] + total[:, k * cond:(k + 1) * cond] + mixed[:, n, :])
        for copy in [c for part in gathers for c in part] + projections + sums + tr_copies:
            copy.wait_send()
        return result

    first = apply(0, [trial_k[g * half + k] for k in range(half)])

    trial = trial_k[...]
    lanes = lax.broadcasted_iota(jnp.int32, (vectors, 128), 1)
    partial = jnp.zeros((vectors, 128), F32)
    for j in range(half):
        lanewise = jnp.sum(trial * first[j][None], axis=1)
        column = jnp.sum(lanewise, axis=1, keepdims=True)
        partial += jnp.where(lanes == g * half + j, column, 0.0)
    dots_send[0] = partial
    dots = to_all(0, dots_send, dots_recv, dots_ssem, dots_rsem)
    for copy in dots:
        copy.start()
    for copy in dots:
        copy.wait()
    for da, dt in everyone:
        partial += dots_recv[0, da * ntr + dt]
    inter = partial / (naux * own_val * ntr * cond)
    dots_send[1] = inter
    core_dots = pltpu.make_async_remote_copy(
        src_ref=dots_send.at[1], dst_ref=core_recv,
        send_sem=core_ssem.at[0], recv_sem=core_rsem.at[0],
        device_id={"grp": 1 - g}, device_id_type=MESH)
    core_dots.start()

    correction = []
    for j in range(half):
        column = jnp.sum(jnp.where(lanes == g * half + j, inter, 0.0), axis=1, keepdims=True)
        fitted = trial_k[0] * column[0:1, :]
        for k in range(1, vectors):
            fitted += trial_k[k] * column[k:k + 1, :]
        correction.append((first[j] - fitted) / gap)

    second = apply(1, correction)
    for k in range(half):
        final_send[k] = second[k]
        out_ref[g * half + k] = second[k]
    final_copy = pltpu.make_async_remote_copy(
        src_ref=final_send, dst_ref=final_recv,
        send_sem=core_ssem.at[1], recv_sem=core_rsem.at[1],
        device_id={"grp": 1 - g}, device_id_type=MESH)
    final_copy.start()
    core_dots.wait()
    inter_ref[...] = (dots_send[1] + core_recv[...])[:, :vectors]
    final_copy.wait()
    for k in range(half):
        out_ref[(1 - g) * half + k] = final_recv[k]


def finish(applied_ref, inter_ref, out_ref, inter_out_ref):
    for k in range(applied_ref.shape[0]):
        out_ref[:, k, :] = applied_ref[k]
    inter_out_ref[...] = inter_ref[...]


def body(naux, ntr, trial_vectors, energy_val, energy_cond, coef_occ, coef_virt, pair_coef, live_aux):
    own_val, vectors, cond = trial_vectors.shape
    slots, val, _ = coef_occ.shape
    naux_all = pair_coef.shape[2]
    half = vectors // 2
    groups = GROUPS
    size = half // groups
    peers = naux * ntr
    vmem = pl.BlockSpec(memory_space=pltpu.VMEM)
    hbm = pl.BlockSpec(memory_space=pl.ANY)
    dma = pltpu.SemaphoreType.DMA
    scratch = [
        pltpu.VMEM(coef_occ.shape, BF16),
        pltpu.VMEM(coef_virt.shape, BF16),
        pltpu.VMEM(pair_coef.shape, BF16),
        pltpu.VMEM((groups, slots // CHUNK, size * val, CHUNK * cond), BF16),
        pltpu.VMEM((size * val, cond), F32),
        pltpu.VMEM((val, size * cond), F32),
        pltpu.VMEM((own_val, half, cond), F32),
        pltpu.VMEM((vectors, own_val, cond), F32),
        pltpu.VMEM((2, groups, own_val, size * cond), BF16),
        pltpu.VMEM((2, groups, naux, own_val, size * cond), BF16),
        pltpu.VMEM((2, half, naux_all), BF16),
        pltpu.VMEM((2, peers, half, naux_all), BF16),
        pltpu.VMEM((2, groups, size * val, cond), BF16),
        pltpu.VMEM((2, groups, size * val, cond), BF16),
        pltpu.VMEM((2, groups, naux, own_val, size * cond), BF16),
        pltpu.VMEM((2, groups, naux, own_val, size * cond), BF16),
        pltpu.VMEM((2, vectors, 128), F32),
        pltpu.VMEM((1, peers, vectors, 128), F32),
        pltpu.VMEM((vectors, 128), F32),
        pltpu.VMEM((half, own_val, cond), F32),
        pltpu.VMEM((half, own_val, cond), F32),
        dma((3,)),
        dma((2, groups, naux)), dma((2, groups, naux)),
        dma((2, peers)), dma((2, peers)),
        dma((2, groups)), dma((2, groups)),
        dma((2, groups, naux)), dma((2, groups, naux)),
        dma((1, peers)), dma((1, peers)),
        dma((2,)), dma((2,)),
    ]
    applied, intersection = pl.pallas_call(
        functools.partial(kernel, naux, ntr, groups),
        out_shape=(
            jax.ShapeDtypeStruct((vectors, own_val, cond), F32),
            jax.ShapeDtypeStruct((vectors, vectors), F32),
        ),
        in_specs=[vmem, vmem, vmem, vmem, hbm, hbm, hbm],
        out_specs=(vmem, vmem),
        scratch_shapes=scratch,
        compiler_params=pltpu.CompilerParams(
            collective_id=0, has_side_effects=True, vmem_limit_bytes=56 * 1024 * 1024
        ),
    )(
        live_aux.reshape(1, 1), trial_vectors, energy_val.reshape(1, -1),
        energy_cond.reshape(1, -1), coef_occ, coef_virt, pair_coef,
    )
    return pl.pallas_call(
        finish,
        out_shape=(
            jax.ShapeDtypeStruct(trial_vectors.shape, F32),
            jax.ShapeDtypeStruct((vectors, vectors), F32),
        ),
        in_specs=[vmem, vmem],
        out_specs=(vmem, vmem),
    )(applied, intersection)


def solution(mesh):
    in_specs = (
        P("aux", None, "tr"),
        P("aux"),
        P("tr"),
        P("aux", None, None),
        P("aux", "tr", None),
        P("aux", "tr", None),
        P("aux"),
    )
    out_specs = (P("aux", None, "tr"), P())
    sizes = (mesh.shape["aux"], mesh.shape["tr"])
    return jax.shard_map(
        functools.partial(body, *sizes), mesh=mesh, in_specs=in_specs, out_specs=out_specs, check_vma=False
    )
```

profile of v0, /device:TPU:0, one launch (start us, length us, event | category | flops | bytes accessed | tf_op | source)
XLA Modules:
  0.0 56.4 jit_solution(16120445365525724211)
XLA Ops:
  1.3 53.6 %shard_map.86 = (f32[8,8,256]{2,1,0:T(8,128)}, f32[8,8]{1,0:T(8,128)}) custom-call(s32[1,1]{1,0:T(1,128)} %bitcast.3.live_ref, f32[8,8,256]{2,1,0:T(8,128)} %trial_ref.1, f32[1,8]{1,0:T(1,128)} %bitcast.5, f32[1,256]{1,0:T(1,128)} %bitcast.4, bf16[64,64,64]{2,1,0:T(8,128)(2,1)} %occ_hbm.1, bf16[64,256,512]{2,1,0:T(8,128)(2,1)} %virt_hbm.1, ...), custom_call_target="tpu_custom_call" | custom-call | tf_op jit(solution)/shard_map/pallas_call | solution.py:292
  54.9 1.5 %shard_map.87 = (f32[8,8,256]{2,1,0:T(8,128)}, f32[8,8]{1,0:T(8,128)}) custom-call(f32[8,8,256]{2,1,0:T(8,128)} %get-tuple-element.4.applied_ref, f32[8,8]{1,0:T(8,128)} %get-tuple-element.5.inter_ref), custom_call_target="tpu_custom_call" | custom-call | tf_op jit(solution)/shard_map/pallas_call | solution.py:308
where the time goes:
time: 56.6 us; the launch traced here: 56.4 us
  Pallas kernels  55.1 us (97%)
  between operations  1.29 us (2%)
    pallas_call x1, Pallas kernels, body(): pl.pallas_call(functools.partial(kernel, naux, ntr, groups), out_shape=(j...  53.6 us
    pallas_call x1, Pallas kernels, body(): pl.pallas_call(finish, out_shape=(jax.ShapeDtypeStruct(trial_vectors.shap...  1.5 us

commit v1 on v0

v1 whole, which is shorter than its diff:
```python
import contextlib
import functools

import jax
import jax.numpy as jnp
from jax import lax
from jax.experimental import pallas as pl
from jax.experimental.pallas import tpu as pltpu
from jax.sharding import PartitionSpec as P

F32 = jnp.float32
BF16 = jnp.bfloat16
CHUNK = 32
BLEND = 32
LANES = 128
MESH = pl.DeviceIdType.MESH


def scope(name):
    return contextlib.nullcontext()


def kernel(
    naux, ntr,
    live_ref, trial_ref, val_ref, cond_ref, occ_hbm, virt_hbm, pair_hbm,
    out_ref, inter_ref,
    occ, virt, pair, blended, acc, mixed, trial_k,
    block_send, block_recv, mate_recv, proj_send, proj_recv, tr_send, tr_recv,
    sum_send, sum_recv, dots_send, dots_recv, core_recv, final_send, final_recv,
    load_sem, block_ssem, block_rsem, mate_sem, proj_ssem, proj_rsem,
    tr_ssem, tr_rsem, sum_ssem, sum_rsem, dots_ssem, dots_rsem, core_ssem, core_rsem,
):
    g = lax.axis_index("grp")
    a = lax.axis_index("aux")
    t = lax.axis_index("tr")
    own_val, vectors, cond = trial_ref.shape
    half = vectors // 2
    slots, val, _ = occ.shape

    pair_copy = pltpu.make_async_copy(pair_hbm, pair, load_sem.at[1])
    occ_copy = pltpu.make_async_copy(occ_hbm, occ, load_sem.at[0])
    virt_copy = pltpu.make_async_copy(virt_hbm, virt, load_sem.at[2])

    everyone = [(da, dt) for da in range(naux) for dt in range(ntr) if (da, dt) != (0, 0)]

    def peer(da, dt):
        return {"aux": lax.rem(a + da, naux), "tr": lax.rem(t + dt, ntr)}

    barrier = pltpu.get_barrier_semaphore()
    with scope("signals"):
        for da, dt in everyone:
            pl.semaphore_signal(barrier, inc=1, device_id=peer(da, dt), device_id_type=MESH)
        pl.semaphore_signal(barrier, inc=1, device_id={"grp": 1 - g}, device_id_type=MESH)
    pair_copy.start()
    occ_copy.start()
    virt_copy.start()

    with scope("prep"):
        square = (own_val, own_val)
        diagonal = lax.broadcasted_iota(jnp.int32, square, 0) == lax.broadcasted_iota(jnp.int32, square, 1)
        val_column = jnp.sum(jnp.where(diagonal, val_ref[...], 0.0), axis=1, keepdims=True)
        gap = cond_ref[...] - val_column
        for k in range(vectors):
            trial_k[k] = trial_ref[:, k, :]

    def to_all(it, send, recv, ssem, rsem):
        copies = []
        for da, dt in everyone:
            n = da * ntr + dt
            copies.append(pltpu.make_async_remote_copy(
                src_ref=send.at[it], dst_ref=recv.at[it, n],
                send_sem=ssem.at[it, n], recv_sem=rsem.at[it, n],
                device_id=peer(da, dt), device_id_type=MESH))
        return copies

    mate = pltpu.make_async_remote_copy(
        src_ref=block_recv.at[0], dst_ref=mate_recv,
        send_sem=mate_sem.at[0], recv_sem=mate_sem.at[1],
        device_id={"grp": 1 - g}, device_id_type=MESH)

    def contract(cols):
        acc[...] = jnp.zeros_like(acc)

        @pl.loop(0, slots // CHUNK)
        def _(i):
            acc[...] += jnp.dot(
                blended[i], virt[pl.ds(i * CHUNK, CHUNK), :, cols].reshape(CHUNK * cond, cond),
                preferred_element_type=F32)

    lanes = lax.broadcasted_iota(jnp.int32, (vectors, LANES), 1)

    def fold(x):
        return sum(x[:, n * LANES:(n + 1) * LANES] for n in range(cond // LANES))

    def overlaps(local):
        mine = [[fold(local[j] * trial_k[k]) for k in range(vectors)] for j in range(half)]
        for s in range(naux):
            same = block_recv[0, s].astype(F32)
            other = mate_recv[s].astype(F32)
            for j in range(half):
                row = j * val + s * own_val
                part = acc[row:row + own_val, :]
                for k in range(half):
                    where = slice(k * cond, (k + 1) * cond)
                    mine[j][k] += fold(part * jnp.where(g == 0, same[:, where], other[:, where]))
                    mine[j][half + k] += fold(part * jnp.where(g == 0, other[:, where], same[:, where]))
        partial = jnp.zeros((vectors, LANES), F32)
        for j in range(half):
            rows = jnp.concatenate([jnp.sum(m, axis=0, keepdims=True) for m in mine[j]], axis=0)
            partial += jnp.where(lanes == g * half + j, jnp.sum(rows, axis=1, keepdims=True), 0.0)
        return partial

    def apply(it, x):
        with scope("pack"):
            block = jnp.concatenate(x, axis=1).astype(BF16)
            block_send[it] = block
            block_recv[it, a] = block
        if it == 0:
            with scope("barrier"):
                pl.semaphore_wait(barrier, len(everyone) + 1)
        gathers = []
        with scope("gather_issue"):
            for d in range(1, naux):
                copy = pltpu.make_async_remote_copy(
                    src_ref=block_send.at[it], dst_ref=block_recv.at[it, a],
                    send_sem=block_ssem.at[it, d], recv_sem=block_rsem.at[it, d],
                    device_id=peer(d, 0), device_id_type=MESH)
                copy.start()
                gathers.append(copy)

        with scope("project"):
            if it == 0:
                pair_copy.wait()
            for k in range(half):
                mixed[:, k, :] = x[k]
            proj = jnp.zeros((half, pair.shape[2]), F32)
            for v in range(own_val):
                proj += jnp.dot(mixed[v].astype(BF16), pair[v], preferred_element_type=F32)
            proj_send[it] = proj.astype(BF16)
            projections = to_all(it, proj_send, proj_recv, proj_ssem, proj_rsem)
            for copy in projections:
                copy.start()

        if it == 0:
            with scope("mask"):
                occ_copy.wait()
                live = live_ref[...]
                step = min(16, slots)

                @pl.loop(0, slots // step)
                def _(i):
                    for q in range(step):
                        p = i * step + q
                        keep = jnp.broadcast_to((p < live).astype(F32), (val, val)).astype(BF16)
                        occ[p] = occ[p] * keep

        with scope("gather_wait"):
            for copy in gathers:
                copy.wait_recv()
        if it == 0:
            mate.start()
        with scope("blend"):
            wide = jnp.concatenate([block_recv[it, s].astype(F32) for s in range(naux)], axis=0).astype(BF16)
            columns = [wide[:, k * cond:(k + 1) * cond] for k in range(half)]

            @pl.loop(0, slots // BLEND)
            def _(i):
                rows = occ[pl.ds(i * BLEND, BLEND)].reshape(BLEND * val, val)
                for k in range(half):
                    b = jnp.dot(rows, columns[k], preferred_element_type=F32).astype(BF16)
                    for q in range(BLEND):
                        blended[i * (BLEND // CHUNK) + q // CHUNK, k * val:(k + 1) * val,
                                (q % CHUNK) * cond:(q % CHUNK + 1) * cond] = b[q * val:(q + 1) * val]

        if it == 0:
            with scope("virt_wait"):
                virt_copy.wait()
        tr_copy = pltpu.make_async_remote_copy(
            src_ref=tr_send.at[it], dst_ref=tr_recv.at[it],
            send_sem=tr_ssem.at[it], recv_sem=tr_rsem.at[it],
            device_id=peer(0, 1), device_id_type=MESH)

        with scope("contract"):
            @pl.loop(0, 2)
            def _(j):
                start = pl.multiple_of(lax.rem(t + 1 + j, ntr) * cond, cond)
                contract(pl.ds(start, cond))

                @pl.when(j == 0)
                def _():
                    tr_send[it] = acc[...].astype(BF16)
                    tr_copy.start()

        with scope("exchange"):
            for copy in projections:
                copy.wait_recv()
            proj = proj_send[it].astype(F32)
            for da, dt in everyone:
                proj += proj_recv[it, da * ntr + dt].astype(F32)
            proj_b = proj.astype(BF16)
            for v in range(own_val):
                mixed[v] = lax.dot_general(
                    proj_b, pair[v], (((1,), (1,)), ((), ())), preferred_element_type=F32)
            local = [gap * x[k] + mixed[:, k, :] for k in range(half)]

        with scope("tr_wait"):
            if it == 0:
                mate.wait_recv()
            tr_copy.wait_recv()
        dots = []
        partial = None
        with scope("dots_calc"):
            acc[...] += tr_recv[it].astype(F32)
            if it == 0:
                partial = overlaps(local)
                dots_send[0] = partial
                dots = to_all(0, dots_send, dots_recv, dots_ssem, dots_rsem)
                for copy in dots:
                    copy.start()

        sums = []
        with scope("sum_issue"):
            for s in range(naux):
                for k in range(half):
                    row = k * val + s * own_val
                    sum_send[it, s, :, k * cond:(k + 1) * cond] = acc[row:row + own_val, :].astype(BF16)
            for d in range(1, naux):
                copy = pltpu.make_async_remote_copy(
                    src_ref=sum_send.at[it, lax.rem(a + d, naux)], dst_ref=sum_recv.at[it, d],
                    send_sem=sum_ssem.at[it, d], recv_sem=sum_rsem.at[it, d],
                    device_id=peer(d, 0), device_id_type=MESH)
                copy.start()
                sums.append(copy)
        with scope("sum_wait"):
            for copy in sums:
                copy.wait_recv()
        with scope("combine"):
            total = sum_send[it, a].astype(F32)
            for d in range(1, naux):
                total += sum_recv[it, d].astype(F32)
            result = [local[k] + total[:, k * cond:(k + 1) * cond] for k in range(half)]
        sent = gathers + projections + sums + [tr_copy] + ([mate] if it == 0 else [])
        return result, partial, dots, sent

    first, partial, dots, sent = apply(0, [trial_k[g * half + k] for k in range(half)])

    with scope("dots_wait"):
        for copy in dots:
            copy.wait_recv()
    with scope("correct"):
        for da, dt in everyone:
            partial += dots_recv[0, da * ntr + dt]
        inter = partial / (naux * own_val * ntr * cond)
        dots_send[1] = inter
        core_dots = pltpu.make_async_remote_copy(
            src_ref=dots_send.at[1], dst_ref=core_recv,
            send_sem=core_ssem.at[0], recv_sem=core_rsem.at[0],
            device_id={"grp": 1 - g}, device_id_type=MESH)
        core_dots.start()

        correction = []
        for j in range(half):
            column = jnp.sum(jnp.where(lanes == g * half + j, inter, 0.0), axis=1, keepdims=True)
            fitted = trial_k[0] * column[0:1, :]
            for k in range(1, vectors):
                fitted += trial_k[k] * column[k:k + 1, :]
            correction.append((first[j] - fitted) / gap)

    second, _, _, sent_second = apply(1, correction)
    with scope("final_pack"):
        for k in range(half):
            final_send[k] = second[k]
        final_copy = pltpu.make_async_remote_copy(
            src_ref=final_send, dst_ref=final_recv,
            send_sem=core_ssem.at[1], recv_sem=core_rsem.at[1],
            device_id={"grp": 1 - g}, device_id_type=MESH)
        final_copy.start()
        for k in range(half):
            out_ref[g * half + k] = second[k]
    with scope("final_sends"):
        core_dots.wait()
        inter_ref[...] = (dots_send[1] + core_recv[...])[:, :vectors]
        for copy in sent + dots + sent_second:
            copy.wait_send()
    with scope("final_wait"):
        final_copy.wait()
    with scope("final_store"):
        for k in range(half):
            out_ref[(1 - g) * half + k] = final_recv[k]


def finish(applied_ref, inter_ref, out_ref, inter_out_ref):
    for k in range(applied_ref.shape[0]):
        out_ref[:, k, :] = applied_ref[k]
    inter_out_ref[...] = inter_ref[...]


def body(naux, ntr, trial_vectors, energy_val, energy_cond, coef_occ, coef_virt, pair_coef, live_aux):
    own_val, vectors, cond = trial_vectors.shape
    slots, val, _ = coef_occ.shape
    naux_all = pair_coef.shape[2]
    half = vectors // 2
    peers = naux * ntr
    vmem = pl.BlockSpec(memory_space=pltpu.VMEM)
    hbm = pl.BlockSpec(memory_space=pl.ANY)
    dma = pltpu.SemaphoreType.DMA
    scratch = [
        pltpu.VMEM(coef_occ.shape, BF16),
        pltpu.VMEM(coef_virt.shape, BF16),
        pltpu.VMEM(pair_coef.shape, BF16),
        pltpu.VMEM((slots // CHUNK, half * val, CHUNK * cond), BF16),
        pltpu.VMEM((half * val, cond), F32),
        pltpu.VMEM((own_val, half, cond), F32),
        pltpu.VMEM((vectors, own_val, cond), F32),
        pltpu.VMEM((2, own_val, half * cond), BF16),
        pltpu.VMEM((2, naux, own_val, half * cond), BF16),
        pltpu.VMEM((naux, own_val, half * cond), BF16),
        pltpu.VMEM((2, half, naux_all), BF16),
        pltpu.VMEM((2, peers, half, naux_all), BF16),
        pltpu.VMEM((2, half * val, cond), BF16),
        pltpu.VMEM((2, half * val, cond), BF16),
        pltpu.VMEM((2, naux, own_val, half * cond), BF16),
        pltpu.VMEM((2, naux, own_val, half * cond), BF16),
        pltpu.VMEM((2, vectors, LANES), F32),
        pltpu.VMEM((1, peers, vectors, LANES), F32),
        pltpu.VMEM((vectors, LANES), F32),
        pltpu.VMEM((half, own_val, cond), F32),
        pltpu.VMEM((half, own_val, cond), F32),
        dma((3,)),
        dma((2, naux)), dma((2, naux)),
        dma((2,)),
        dma((2, peers)), dma((2, peers)),
        dma((2,)), dma((2,)),
        dma((2, naux)), dma((2, naux)),
        dma((1, peers)), dma((1, peers)),
        dma((2,)), dma((2,)),
    ]
    applied, intersection = pl.pallas_call(
        functools.partial(kernel, naux, ntr),
        out_shape=(
            jax.ShapeDtypeStruct((vectors, own_val, cond), F32),
            jax.ShapeDtypeStruct((vectors, vectors), F32),
        ),
        in_specs=[vmem, vmem, vmem, vmem, hbm, hbm, hbm],
        out_specs=(vmem, vmem),
        scratch_shapes=scratch,
        compiler_params=pltpu.CompilerParams(
            collective_id=0, has_side_effects=True, vmem_limit_bytes=56 * 1024 * 1024
        ),
    )(
        live_aux.reshape(1, 1), trial_vectors, energy_val.reshape(1, -1),
        energy_cond.reshape(1, -1), coef_occ, coef_virt, pair_coef,
    )
    return pl.pallas_call(
        finish,
        out_shape=(
            jax.ShapeDtypeStruct(trial_vectors.shape, F32),
            jax.ShapeDtypeStruct((vectors, vectors), F32),
        ),
        in_specs=[vmem, vmem],
        out_specs=(vmem, vmem),
    )(applied, intersection)


def solution(mesh):
    in_specs = (
        P("aux", None, "tr"),
        P("aux"),
        P("tr"),
        P("aux", None, None),
        P("aux", "tr", None),
        P("aux", "tr", None),
        P("aux"),
    )
    out_specs = (P("aux", None, "tr"), P())
    sizes = (mesh.shape["aux"], mesh.shape["tr"])
    return jax.shard_map(
        functools.partial(body, *sizes), mesh=mesh, in_specs=in_specs, out_specs=out_specs, check_vma=False
    )
```

time: 56.6 us -> 51.9 us (0.917)
  Pallas kernels: 55.1 us -> 50.4 us
    pallas_call x1, Pallas kernels: 53.6 us -> 48.9 us  [body(): pl.pallas_call(functools.partial(kernel, naux, ntr), out_shape=(jax.Shape...]
where the time goes in v1:
time: 51.9 us; the launch traced here: 51.7 us
  Pallas kernels  50.4 us (97%)
  between operations  1.29 us (2%)
    pallas_call x1, Pallas kernels, body(): pl.pallas_call(functools.partial(kernel, naux, ntr), out_shape=(jax.Shape...  48.9 us
    pallas_call x1, Pallas kernels, body(): pl.pallas_call(finish, out_shape=(jax.ShapeDtypeStruct(trial_vectors.shap...  1.5 us

profile of v1, /device:TPU:0, one launch (start us, length us, event | category | flops | bytes accessed | tf_op | source)
XLA Modules:
  0.0 51.7 jit_solution(8989616990837698601)
XLA Ops:
  1.3 48.9 %shard_map.86 = (f32[8,8,256]{2,1,0:T(8,128)}, f32[8,8]{1,0:T(8,128)}) custom-call(s32[1,1]{1,0:T(1,128)} %bitcast.3.live_ref, f32[8,8,256]{2,1,0:T(8,128)} %trial_ref.1, f32[1,8]{1,0:T(1,128)} %bitcast.5, f32[1,256]{1,0:T(1,128)} %bitcast.4, bf16[64,64,64]{2,1,0:T(8,128)(2,1)} %occ_hbm.1, bf16[64,256,512]{2,1,0:T(8,128)(2,1)} %virt_hbm.1, ...), custom_call_target="tpu_custom_call" | custom-call | tf_op jit(solution)/shard_map/pallas_call | solution.py:338
  50.2 1.5 %shard_map.87 = (f32[8,8,256]{2,1,0:T(8,128)}, f32[8,8]{1,0:T(8,128)}) custom-call(f32[8,8,256]{2,1,0:T(8,128)} %get-tuple-element.4.applied_ref, f32[8,8]{1,0:T(8,128)} %get-tuple-element.5.inter_ref), custom_call_target="tpu_custom_call" | custom-call | tf_op jit(solution)/shard_map/pallas_call | solution.py:354

commit v2 on v1

v2 whole, which is shorter than its diff:
```python
import contextlib
import functools

import jax
import jax.numpy as jnp
from jax import lax
from jax.experimental import pallas as pl
from jax.experimental.pallas import tpu as pltpu
from jax.sharding import PartitionSpec as P

F32 = jnp.float32
BF16 = jnp.bfloat16
CHUNK = 32
BLEND = 32
LANES = 128
MESH = pl.DeviceIdType.MESH


def scope(name):
    return contextlib.nullcontext()


def kernel(
    naux, ntr,
    live_ref, trial_ref, val_ref, cond_ref, occ_hbm, virt_hbm, pair_hbm,
    out_ref, inter_ref,
    occ, virt, pair, blended, acc, mixed, trial_k, own_row,
    block_send, block_recv, cross_recv, mate_recv, proj_send, proj_recv, proj_all, proj_mate,
    sum_send, sum_recv, dots_send, dots_recv, core_recv, final_send, final_recv,
    load_sem, block_ssem, block_rsem, extra_ssem, extra_rsem, proj_ssem, proj_rsem,
    sum_ssem, sum_rsem, dots_ssem, dots_rsem, core_ssem, core_rsem,
):
    g = lax.axis_index("grp")
    a = lax.axis_index("aux")
    t = lax.axis_index("tr")
    own_val, vectors, cond = trial_ref.shape
    half = vectors // 2
    slots, val, _ = occ.shape
    here = a * ntr + t

    pair_copy = pltpu.make_async_copy(pair_hbm, pair, load_sem.at[1])
    occ_copy = pltpu.make_async_copy(occ_hbm, occ, load_sem.at[0])
    virt_copy = pltpu.make_async_copy(virt_hbm, virt, load_sem.at[2])

    everyone = [(da, dt) for da in range(naux) for dt in range(ntr) if (da, dt) != (0, 0)]

    def peer(da, dt):
        return {"aux": lax.rem(a + da, naux), "tr": lax.rem(t + dt, ntr)}

    def send(src, dst, ssem, rsem, device):
        return pltpu.make_async_remote_copy(
            src_ref=src, dst_ref=dst, send_sem=ssem, recv_sem=rsem, device_id=device, device_id_type=MESH)

    mate = {"grp": 1 - g}
    barrier = pltpu.get_barrier_semaphore()
    with scope("signals"):
        for da, dt in everyone:
            pl.semaphore_signal(barrier, inc=1, device_id=peer(da, dt), device_id_type=MESH)
        pl.semaphore_signal(barrier, inc=1, device_id=mate, device_id_type=MESH)
    pair_copy.start()
    occ_copy.start()
    virt_copy.start()

    with scope("prep"):
        square = (own_val, own_val)
        diagonal = lax.broadcasted_iota(jnp.int32, square, 0) == lax.broadcasted_iota(jnp.int32, square, 1)
        val_column = jnp.sum(jnp.where(diagonal, val_ref[...], 0.0), axis=1, keepdims=True)
        gap = cond_ref[...] - val_column
        for k in range(vectors):
            trial_k[k] = trial_ref[:, k, :]

    pairs = half * vectors
    lane = lax.broadcasted_iota(jnp.int32, (vectors, LANES), 1)
    vector = lax.broadcasted_iota(jnp.int32, (vectors, LANES), 0)

    def fold(x):
        return sum(x[:, n * LANES:(n + 1) * LANES] for n in range(x.shape[1] // LANES))

    def row_of(parts):
        rows = jnp.concatenate([jnp.sum(p, axis=0, keepdims=True) for part in parts for p in part], axis=0)
        n = lax.broadcasted_iota(jnp.int32, (pairs, LANES), 0)
        j = n // vectors
        place = j * vectors + lax.rem(n - j * vectors + g * half, vectors)
        spread = lax.broadcasted_iota(jnp.int32, (pairs, LANES), 1) == place
        return jnp.sum(jnp.where(spread, jnp.sum(rows, axis=1, keepdims=True), 0.0), axis=0, keepdims=True)

    def column(row, j):
        return jnp.sum(jnp.where(lane == j * vectors + vector, row, 0.0), axis=1, keepdims=True)

    def contract(cols):
        acc[...] = jnp.zeros_like(acc)

        @pl.loop(0, slots // CHUNK)
        def _(i):
            acc[...] += jnp.dot(
                blended[i], virt[pl.ds(i * CHUNK, CHUNK), :, cols].reshape(CHUNK * cond, cond),
                preferred_element_type=F32)

    def apply(it, x):
        started = []

        def go(copy):
            copy.start()
            started.append(copy)
            return copy

        with scope("pack"):
            block = jnp.concatenate(x, axis=1).astype(BF16)
            block_send[it] = block
            block_recv[it, a] = block
        if it == 0:
            with scope("barrier"):
                pl.semaphore_wait(barrier, len(everyone) + 1)
        with scope("gather_issue"):
            gathers = [
                go(send(block_send.at[it], block_recv.at[it, a], block_ssem.at[it, d], block_rsem.at[it, d], peer(d, 0)))
                for d in range(1, naux)]

        with scope("project"):
            if it == 0:
                pair_copy.wait()
            for k in range(half):
                mixed[:, k, :] = x[k]
            proj = jnp.zeros((half, pair.shape[2]), F32)
            for v in range(own_val):
                proj += jnp.dot(mixed[v].astype(BF16), pair[v], preferred_element_type=F32)
            proj_send[it] = proj.astype(BF16)
            proj_recv[it, here] = proj.astype(BF16)

        if it == 0:
            with scope("mask"):
                occ_copy.wait()
                live = live_ref[...]
                step = min(16, slots)

                @pl.loop(0, slots // step)
                def _(i):
                    for q in range(step):
                        p = i * step + q
                        keep = jnp.broadcast_to((p < live).astype(F32), (val, val)).astype(BF16)
                        occ[p] = occ[p] * keep

                others = [trial_k[lax.rem(g * half + n, vectors)] for n in range(vectors)]
                own_row[...] = row_of([[fold(gap * others[j] * others[n]) for n in range(vectors)] for j in range(half)])

        with scope("gather_wait"):
            for copy in gathers:
                copy.wait_recv()
        if it == 0:
            mate_cross = send(cross_recv, mate_recv.at[1], extra_ssem.at[2], extra_rsem.at[2], mate)
        with scope("proj_issue"):
            projections = []
            for da, dt in everyone:
                n = da * ntr + dt
                projections.append(go(send(
                    proj_send.at[it], proj_recv.at[it, here], proj_ssem.at[it, n], proj_rsem.at[it, n], peer(da, dt))))
            if it == 0:
                mate_own = go(send(block_recv.at[0], mate_recv.at[0], extra_ssem.at[0], extra_rsem.at[0], mate))
                cross = go(send(block_recv.at[0], cross_recv, extra_ssem.at[1], extra_rsem.at[1], peer(0, 1)))
        with scope("blend"):
            wide = jnp.concatenate([block_recv[it, s].astype(F32) for s in range(naux)], axis=0).astype(BF16)
            columns = [wide[:, k * cond:(k + 1) * cond] for k in range(half)]

            @pl.loop(0, slots // BLEND)
            def _(i):
                rows = occ[pl.ds(i * BLEND, BLEND)].reshape(BLEND * val, val)
                for k in range(half):
                    b = jnp.dot(rows, columns[k], preferred_element_type=F32).astype(BF16)
                    for q in range(BLEND):
                        blended[i * (BLEND // CHUNK) + q // CHUNK, k * val:(k + 1) * val,
                                (q % CHUNK) * cond:(q % CHUNK + 1) * cond] = b[q * val:(q + 1) * val]

        if it == 0:
            with scope("virt_wait"):
                virt_copy.wait()

        def sum_copies(dt):
            return [
                send(sum_send.at[it, dt, lax.rem(a + d, naux)], sum_recv.at[it, dt, d],
                     sum_ssem.at[it, dt, d], sum_rsem.at[it, dt, d], peer(d, dt))
                for d in range(1 - dt, naux)]

        with scope("contract"):
            @pl.loop(0, 2)
            def _(j):
                start = pl.multiple_of(lax.rem(t + 1 - j, ntr) * cond, cond)
                contract(pl.ds(start, cond))
                for s in range(naux):
                    for k in range(half):
                        row = k * val + s * own_val
                        sum_send[it, 1 - j, s, :, k * cond:(k + 1) * cond] = acc[row:row + own_val, :].astype(BF16)

                @pl.when(j == 0)
                def _():
                    for copy in sum_copies(1):
                        copy.start()
                    if it == 0:
                        cross.wait_recv()
                        mate_cross.start()

        with scope("sum_issue"):
            for copy in sum_copies(0):
                copy.start()
            sums = sum_copies(1) + sum_copies(0)
            started.extend(sums + ([mate_cross] if it == 0 else []))

        dots = []
        if it == 0:
            with scope("overlap"):
                mate_own.wait_recv()
                mate_cross.wait_recv()
                parts = [[jnp.zeros((own_val, LANES), F32)] * vectors for _ in range(half)]
                for dt in range(2):
                    for s in range(naux):
                        part = sum_send[0, dt, s].astype(F32)
                        same = (block_recv[0, s] if dt == 0 else cross_recv[s]).astype(F32)
                        other = mate_recv[dt, s].astype(F32)
                        both = [y[:, k * cond:(k + 1) * cond] for y in (same, other) for k in range(half)]
                        for j in range(half):
                            mine = part[:, j * cond:(j + 1) * cond]
                            for n in range(vectors):
                                parts[j][n] = parts[j][n] + fold(mine * both[n])
                row = own_row[...] + row_of(parts)
                dots_send[...] = row
                dots_recv[here] = row
            with scope("dots_issue"):
                for da, dt in everyone:
                    n = da * ntr + dt
                    dots.append(go(send(dots_send, dots_recv.at[here], dots_ssem.at[n], dots_rsem.at[n], peer(da, dt))))

        with scope("exchange"):
            for copy in projections:
                copy.wait_recv()
            proj = proj_recv[it, 0].astype(F32)
            for n in range(1, naux * ntr):
                proj += proj_recv[it, n].astype(F32)
            if it == 0:
                proj_all[...] = proj
                mate_proj = go(send(proj_all, proj_mate, extra_ssem.at[3], extra_rsem.at[3], mate))
            proj_b = proj.astype(BF16)
            for v in range(own_val):
                mixed[v] = lax.dot_general(
                    proj_b, pair[v], (((1,), (1,)), ((), ())), preferred_element_type=F32)
            local = [gap * x[k] + mixed[:, k, :] for k in range(half)]

        with scope("sum_wait"):
            for copy in sums:
                copy.wait_recv()
        with scope("combine"):
            total = sum_send[it, 0, a].astype(F32)
            for dt in range(2):
                for d in range(1 - dt, naux):
                    total += sum_recv[it, dt, d].astype(F32)
            result = [local[k] + total[:, k * cond:(k + 1) * cond] for k in range(half)]
        return result, dots, proj_b, mate_proj if it == 0 else None, started

    first, dots, proj_b, mate_proj, started = apply(0, [trial_k[g * half + k] for k in range(half)])

    with scope("dots_wait"):
        mate_proj.wait_recv()
        for copy in dots:
            copy.wait_recv()
    with scope("correct"):
        row = dots_recv[0]
        for n in range(1, naux * ntr):
            row += dots_recv[n]
        both = jnp.concatenate([proj_all[...], proj_mate[...]], axis=0)
        both = jnp.where(g == 0, both, jnp.concatenate([proj_mate[...], proj_all[...]], axis=0))
        inter = []
        for j in range(half):
            exchanged = jnp.sum(fold(both * proj_b[j:j + 1].astype(F32)), axis=1, keepdims=True)
            inter.append((column(row, j) + exchanged) / (naux * own_val * ntr * cond))
        square = jnp.zeros((vectors, LANES), F32)
        for j in range(half):
            square += jnp.where(lane == g * half + j, inter[j], 0.0)
        core_recv[0] = square
        core_dots = send(core_recv.at[0], core_recv.at[1], core_ssem.at[0], core_rsem.at[0], mate)
        core_dots.start()

        correction = []
        for j in range(half):
            fitted = trial_k[0] * inter[j][0:1, :]
            for k in range(1, vectors):
                fitted += trial_k[k] * inter[j][k:k + 1, :]
            correction.append((first[j] - fitted) / gap)

    second, _, _, _, started_second = apply(1, correction)
    with scope("final_pack"):
        for k in range(half):
            final_send[k] = second[k]
        final_copy = send(final_send, final_recv, core_ssem.at[1], core_rsem.at[1], mate)
        final_copy.start()
        for k in range(half):
            out_ref[g * half + k] = second[k]
    with scope("final_sends"):
        core_dots.wait()
        inter_ref[...] = (core_recv[0] + core_recv[1])[:, :vectors]
        for copy in started + started_second:
            copy.wait_send()
    with scope("final_wait"):
        final_copy.wait()
    with scope("final_store"):
        for k in range(half):
            out_ref[(1 - g) * half + k] = final_recv[k]


def finish(applied_ref, inter_ref, out_ref, inter_out_ref):
    for k in range(applied_ref.shape[0]):
        out_ref[:, k, :] = applied_ref[k]
    inter_out_ref[...] = inter_ref[...]


def body(naux, ntr, trial_vectors, energy_val, energy_cond, coef_occ, coef_virt, pair_coef, live_aux):
    own_val, vectors, cond = trial_vectors.shape
    slots, val, _ = coef_occ.shape
    naux_all = pair_coef.shape[2]
    half = vectors // 2
    peers = naux * ntr
    vmem = pl.BlockSpec(memory_space=pltpu.VMEM)
    hbm = pl.BlockSpec(memory_space=pl.ANY)
    dma = pltpu.SemaphoreType.DMA
    block = (own_val, half * cond)
    scratch = [
        pltpu.VMEM(coef_occ.shape, BF16),
        pltpu.VMEM(coef_virt.shape, BF16),
        pltpu.VMEM(pair_coef.shape, BF16),
        pltpu.VMEM((slots // CHUNK, half * val, CHUNK * cond), BF16),
        pltpu.VMEM((half * val, cond), F32),
        pltpu.VMEM((own_val, half, cond), F32),
        pltpu.VMEM((vectors, own_val, cond), F32),
        pltpu.VMEM((1, LANES), F32),
        pltpu.VMEM((2, *block), BF16),
        pltpu.VMEM((2, naux, *block), BF16),
        pltpu.VMEM((naux, *block), BF16),
        pltpu.VMEM((2, naux, *block), BF16),
        pltpu.VMEM((2, half, naux_all), BF16),
        pltpu.VMEM((2, peers, half, naux_all), BF16),
        pltpu.VMEM((half, naux_all), F32),
        pltpu.VMEM((half, naux_all), F32),
        pltpu.VMEM((2, 2, naux, *block), BF16),
        pltpu.VMEM((2, 2, naux, *block), BF16),
        pltpu.VMEM((1, LANES), F32),
        pltpu.VMEM((peers, 1, LANES), F32),
        pltpu.VMEM((2, vectors, LANES), F32),
        pltpu.VMEM((half, own_val, cond), F32),
        pltpu.VMEM((half, own_val, cond), F32),
        dma((3,)),
        dma((2, naux)), dma((2, naux)),
        dma((4,)), dma((4,)),
        dma((2, peers)), dma((2, peers)),
        dma((2, 2, naux)), dma((2, 2, naux)),
        dma((peers,)), dma((peers,)),
        dma((2,)), dma((2,)),
    ]
    applied, intersection = pl.pallas_call(
        functools.partial(kernel, naux, ntr),
        out_shape=(
            jax.ShapeDtypeStruct((vectors, own_val, cond), F32),
            jax.ShapeDtypeStruct((vectors, vectors), F32),
        ),
        in_specs=[vmem, vmem, vmem, vmem, hbm, hbm, hbm],
        out_specs=(vmem, vmem),
        scratch_shapes=scratch,
        compiler_params=pltpu.CompilerParams(
            collective_id=0, has_side_effects=True, vmem_limit_bytes=56 * 1024 * 1024
        ),
    )(
        live_aux.reshape(1, 1), trial_vectors, energy_val.reshape(1, -1),
        energy_cond.reshape(1, -1), coef_occ, coef_virt, pair_coef,
    )
    return pl.pallas_call(
        finish,
        out_shape=(
            jax.ShapeDtypeStruct(trial_vectors.shape, F32),
            jax.ShapeDtypeStruct((vectors, vectors), F32),
        ),
        in_specs=[vmem, vmem],
        out_specs=(vmem, vmem),
    )(applied, intersection)


def solution(mesh):
    in_specs = (
        P("aux", None, "tr"),
        P("aux"),
        P("tr"),
        P("aux", None, None),
        P("aux", "tr", None),
        P("aux", "tr", None),
        P("aux"),
    )
    out_specs = (P("aux", None, "tr"), P())
    sizes = (mesh.shape["aux"], mesh.shape["tr"])
    return jax.shard_map(
        functools.partial(body, *sizes), mesh=mesh, in_specs=in_specs, out_specs=out_specs, check_vma=False
    )
```

time: 51.9 us -> 49.1 us (0.946)
  Pallas kernels: 50.4 us -> 47.6 us
    pallas_call x1, Pallas kernels: 48.9 us -> 46.1 us  [body(): pl.pallas_call(functools.partial(kernel, naux, ntr), out_shape=(jax.Shape...]
where the time goes in v2:
time: 49.1 us; the launch traced here: 48.9 us
  Pallas kernels  47.6 us (97%)
  between operations  1.29 us (3%)
    pallas_call x1, Pallas kernels, body(): pl.pallas_call(functools.partial(kernel, naux, ntr), out_shape=(jax.Shape...  46.1 us
    pallas_call x1, Pallas kernels, body(): pl.pallas_call(finish, out_shape=(jax.ShapeDtypeStruct(trial_vectors.shap...  1.5 us

profile of v2, /device:TPU:0, one launch (start us, length us, event | category | flops | bytes accessed | tf_op | source)
XLA Modules:
  0.0 48.9 jit_solution(14552909737423873043)
XLA Ops:
  1.3 46.1 %shard_map.86 = (f32[8,8,256]{2,1,0:T(8,128)}, f32[8,8]{1,0:T(8,128)}) custom-call(s32[1,1]{1,0:T(1,128)} %bitcast.3.live_ref, f32[8,8,256]{2,1,0:T(8,128)} %trial_ref.1, f32[1,8]{1,0:T(1,128)} %bitcast.5, f32[1,256]{1,0:T(1,128)} %bitcast.4, bf16[64,64,64]{2,1,0:T(8,128)(2,1)} %occ_hbm.1, bf16[64,256,512]{2,1,0:T(8,128)(2,1)} %virt_hbm.1, ...), custom_call_target="tpu_custom_call" | custom-call | tf_op jit(solution)/shard_map/pallas_call | solution.py:355
  47.4 1.5 %shard_map.87 = (f32[8,8,256]{2,1,0:T(8,128)}, f32[8,8]{1,0:T(8,128)}) custom-call(f32[8,8,256]{2,1,0:T(8,128)} %get-tuple-element.4.applied_ref, f32[8,8]{1,0:T(8,128)} %get-tuple-element.5.inter_ref), custom_call_target="tpu_custom_call" | custom-call | tf_op jit(solution)/shard_map/pallas_call | solution.py:371

commit v3 on v2

--- a/solution.py
+++ b/solution.py
@@ -22,13 +22,12 @@
 
 def kernel(
     naux, ntr,
-    live_ref, trial_ref, val_ref, cond_ref, occ_hbm, virt_hbm, pair_hbm,
+    live_ref, trial_hbm, val_hbm, cond_hbm, occ_hbm, virt_hbm, pair_hbm,
     out_ref, inter_ref,
-    occ, virt, pair, blended, acc, mixed, trial_k, own_row,
+    trial_ref, val_ref, cond_ref, occ, virt, pair, blended, acc, mixed, trial_k, own_row,
     block_send, block_recv, cross_recv, mate_recv, proj_send, proj_recv, proj_all, proj_mate,
     sum_send, sum_recv, dots_send, dots_recv, core_recv, final_send, final_recv,
-    load_sem, block_ssem, block_rsem, extra_ssem, extra_rsem, proj_ssem, proj_rsem,
-    sum_ssem, sum_rsem, dots_ssem, dots_rsem, core_ssem, core_rsem,
+    load_sem, block_sem, proj_sem, sum_sem, dots_sem, extra_ssem, extra_rsem,
 ):
     g = lax.axis_index("grp")
     a = lax.axis_index("aux")
@@ -38,9 +37,12 @@
     slots, val, _ = occ.shape
     here = a * ntr + t
 
-    pair_copy = pltpu.make_async_copy(pair_hbm, pair, load_sem.at[1])
-    occ_copy = pltpu.make_async_copy(occ_hbm, occ, load_sem.at[0])
-    virt_copy = pltpu.make_async_copy(virt_hbm, virt, load_sem.at[2])
+    arrays = ((trial_hbm, trial_ref), (val_hbm, val_ref), (cond_hbm, cond_ref),
+              (pair_hbm, pair), (occ_hbm, occ), (virt_hbm, virt))
+    loads = [pltpu.make_async_copy(src, dst, load_sem.at[n]) for n, (src, dst) in enumerate(arrays)]
+    pair_copy, occ_copy, virt_copy = loads[3:]
+    for copy in loads[:3]:
+        copy.start()
 
     everyone = [(da, dt) for da in range(naux) for dt in range(ntr) if (da, dt) != (0, 0)]
 
@@ -50,6 +52,9 @@
     def send(src, dst, ssem, rsem, device):
         return pltpu.make_async_remote_copy(
             src_ref=src, dst_ref=dst, send_sem=ssem, recv_sem=rsem, device_id=device, device_id_type=MESH)
+
+    def drain(refs, sem):
+        return pltpu.make_async_copy(refs, refs, sem).wait
 
     mate = {"grp": 1 - g}
     barrier = pltpu.get_barrier_semaphore()
@@ -57,11 +62,12 @@
         for da, dt in everyone:
             pl.semaphore_signal(barrier, inc=1, device_id=peer(da, dt), device_id_type=MESH)
         pl.semaphore_signal(barrier, inc=1, device_id=mate, device_id_type=MESH)
-    pair_copy.start()
-    occ_copy.start()
-    virt_copy.start()
+    for copy in loads[3:]:
+        copy.start()
 
     with scope("prep"):
+        for copy in loads[:3]:
+            copy.wait()
         square = (own_val, own_val)
         diagonal = lax.broadcasted_iota(jnp.int32, square, 0) == lax.broadcasted_iota(jnp.int32, square, 1)
         val_column = jnp.sum(jnp.where(diagonal, val_ref[...], 0.0), axis=1, keepdims=True)
@@ -97,11 +103,11 @@
                 preferred_element_type=F32)
 
     def apply(it, x):
-        started = []
+        finals = []
 
         def go(copy):
             copy.start()
-            started.append(copy)
+            finals.append(copy.wait_send)
             return copy
 
         with scope("pack"):
@@ -112,9 +118,10 @@
             with scope("barrier"):
                 pl.semaphore_wait(barrier, len(everyone) + 1)
         with scope("gather_issue"):
-            gathers = [
-                go(send(block_send.at[it], block_recv.at[it, a], block_ssem.at[it, d], block_rsem.at[it, d], peer(d, 0)))
-                for d in range(1, naux)]
+            for d in range(1, naux):
+                send(block_send.at[it], block_recv.at[it, a], block_sem.at[0, it], block_sem.at[1, it], peer(d, 0)).start()
+            blocks = block_recv.at[it, pl.ds(0, naux - 1)]
+            finals.append(drain(blocks, block_sem.at[0, it]))
 
         with scope("project"):
             if it == 0:
@@ -130,30 +137,28 @@
         if it == 0:
             with scope("mask"):
                 occ_copy.wait()
-                live = live_ref[...]
+                live = live_ref[0]
                 step = min(16, slots)
 
                 @pl.loop(0, slots // step)
                 def _(i):
                     for q in range(step):
                         p = i * step + q
-                        keep = jnp.broadcast_to((p < live).astype(F32), (val, val)).astype(BF16)
+                        keep = jnp.full((val, val), jnp.where(p < live, 1.0, 0.0), F32).astype(BF16)
                         occ[p] = occ[p] * keep
 
                 others = [trial_k[lax.rem(g * half + n, vectors)] for n in range(vectors)]
                 own_row[...] = row_of([[fold(gap * others[j] * others[n]) for n in range(vectors)] for j in range(half)])
 
         with scope("gather_wait"):
-            for copy in gathers:
-                copy.wait_recv()
+            drain(blocks, block_sem.at[1, it])()
         if it == 0:
             mate_cross = send(cross_recv, mate_recv.at[1], extra_ssem.at[2], extra_rsem.at[2], mate)
         with scope("proj_issue"):
-            projections = []
             for da, dt in everyone:
-                n = da * ntr + dt
-                projections.append(go(send(
-                    proj_send.at[it], proj_recv.at[it, here], proj_ssem.at[it, n], proj_rsem.at[it, n], peer(da, dt))))
+                send(proj_send.at[it], proj_recv.at[it, here], proj_sem.at[0, it], proj_sem.at[1, it], peer(da, dt)).start()
+            projections = proj_recv.at[it, pl.ds(0, len(everyone))]
+            finals.append(drain(projections, proj_sem.at[0, it]))
             if it == 0:
                 mate_own = go(send(block_recv.at[0], mate_recv.at[0], extra_ssem.at[0], extra_rsem.at[0], mate))
                 cross = go(send(block_recv.at[0], cross_recv, extra_ssem.at[1], extra_rsem.at[1], peer(0, 1)))
@@ -176,8 +181,8 @@
 
         def sum_copies(dt):
             return [
-                send(sum_send.at[it, dt, lax.rem(a + d, naux)], sum_recv.at[it, dt, d],
-                     sum_ssem.at[it, dt, d], sum_rsem.at[it, dt, d], peer(d, dt))
+                send(sum_send.at[it, dt, lax.rem(a + d, naux)], sum_recv.at[it, dt * naux + d],
+                     sum_sem.at[0, it], sum_sem.at[1, it], peer(d, dt))
                 for d in range(1 - dt, naux)]
 
         with scope("contract"):
@@ -201,10 +206,11 @@
         with scope("sum_issue"):
             for copy in sum_copies(0):
                 copy.start()
-            sums = sum_copies(1) + sum_copies(0)
-            started.extend(sums + ([mate_cross] if it == 0 else []))
-
-        dots = []
+            sums = sum_recv.at[it, pl.ds(1, len(everyone))]
+            finals.append(drain(sums, sum_sem.at[0, it]))
+            if it == 0:
+                finals.append(mate_cross.wait_send)
+
         if it == 0:
             with scope("overlap"):
                 mate_own.wait_recv()
@@ -225,12 +231,10 @@
                 dots_recv[here] = row
             with scope("dots_issue"):
                 for da, dt in everyone:
-                    n = da * ntr + dt
-                    dots.append(go(send(dots_send, dots_recv.at[here], dots_ssem.at[n], dots_rsem.at[n], peer(da, dt))))
+                    send(dots_send, dots_recv.at[here], dots_sem.at[0], dots_sem.at[1], peer(da, dt)).start()
 
         with scope("exchange"):
-            for copy in projections:
-                copy.wait_recv()
+            drain(projections, proj_sem.at[1, it])()
             proj = proj_recv[it, 0].astype(F32)
             for n in range(1, naux * ntr):
                 proj += proj_recv[it, n].astype(F32)
@@ -244,22 +248,21 @@
             local = [gap * x[k] + mixed[:, k, :] for k in range(half)]
 
         with scope("sum_wait"):
-            for copy in sums:
-                copy.wait_recv()
+            drain(sums, sum_sem.at[1, it])()
         with scope("combine"):
             total = sum_send[it, 0, a].astype(F32)
-            for dt in range(2):
-                for d in range(1 - dt, naux):
-                    total += sum_recv[it, dt, d].astype(F32)
+            for n in range(1, naux * ntr):
+                total += sum_recv[it, n].astype(F32)
             result = [local[k] + total[:, k * cond:(k + 1) * cond] for k in range(half)]
-        return result, dots, proj_b, mate_proj if it == 0 else None, started
-
-    first, dots, proj_b, mate_proj, started = apply(0, [trial_k[g * half + k] for k in range(half)])
+        return result, proj_b, mate_proj if it == 0 else None, finals
+
+    first, proj_b, mate_proj, finals = apply(0, [trial_k[g * half + k] for k in range(half)])
 
     with scope("dots_wait"):
         mate_proj.wait_recv()
-        for copy in dots:
-            copy.wait_recv()
+        dots = dots_recv.at[pl.ds(0, len(everyone))]
+        drain(dots, dots_sem.at[1])()
+        finals.append(drain(dots, dots_sem.at[0]))
     with scope("correct"):
         row = dots_recv[0]
         for n in range(1, naux * ntr):
@@ -274,7 +277,7 @@
         for j in range(half):
             square += jnp.where(lane == g * half + j, inter[j], 0.0)
         core_recv[0] = square
-        core_dots = send(core_recv.at[0], core_recv.at[1], core_ssem.at[0], core_rsem.at[0], mate)
+        core_dots = send(core_recv.at[0], core_recv.at[1], extra_ssem.at[4], extra_rsem.at[4], mate)
         core_dots.start()
 
         correction = []
@@ -284,19 +287,19 @@
                 fitted += trial_k[k] * inter[j][k:k + 1, :]
             correction.append((first[j] - fitted) / gap)
 
-    second, _, _, _, started_second = apply(1, correction)
+    second, _, _, more = apply(1, correction)
     with scope("final_pack"):
         for k in range(half):
             final_send[k] = second[k]
-        final_copy = send(final_send, final_recv, core_ssem.at[1], core_rsem.at[1], mate)
+        final_copy = send(final_send, final_recv, extra_ssem.at[5], extra_rsem.at[5], mate)
         final_copy.start()
         for k in range(half):
             out_ref[g * half + k] = second[k]
     with scope("final_sends"):
         core_dots.wait()
         inter_ref[...] = (core_recv[0] + core_recv[1])[:, :vectors]
-        for copy in started + started_second:
-            copy.wait_send()
+        for wait in finals + more:
+            wait()
     with scope("final_wait"):
         final_copy.wait()
     with scope("final_store"):
@@ -317,10 +320,13 @@
     half = vectors // 2
     peers = naux * ntr
     vmem = pl.BlockSpec(memory_space=pltpu.VMEM)
-    hbm = pl.BlockSpec(memory_space=pl.ANY)
+    hbm = pl.BlockSpec(memory_space=pltpu.HBM)
     dma = pltpu.SemaphoreType.DMA
     block = (own_val, half * cond)
     scratch = [
+        pltpu.VMEM(trial_vectors.shape, F32),
+        pltpu.VMEM((1, own_val), F32),
+        pltpu.VMEM((1, cond), F32),
         pltpu.VMEM(coef_occ.shape, BF16),
         pltpu.VMEM(coef_virt.shape, BF16),
         pltpu.VMEM(pair_coef.shape, BF16),
@@ -337,20 +343,20 @@
         pltpu.VMEM((2, peers, half, naux_all), BF16),
         pltpu.VMEM((half, naux_all), F32),
         pltpu.VMEM((half, naux_all), F32),
-        pltpu.VMEM((2, 2, naux, *block), BF16),
-        pltpu.VMEM((2, 2, naux, *block), BF16),
+        pltpu.VMEM((2, ntr, naux, *block), BF16),
+        pltpu.VMEM((2, peers, *block), BF16),
         pltpu.VMEM((1, LANES), F32),
         pltpu.VMEM((peers, 1, LANES), F32),
         pltpu.VMEM((2, vectors, LANES), F32),
         pltpu.VMEM((half, own_val, cond), F32),
         pltpu.VMEM((half, own_val, cond), F32),
-        dma((3,)),
-        dma((2, naux)), dma((2, naux)),
-        dma((4,)), dma((4,)),
-        dma((2, peers)), dma((2, peers)),
-        dma((2, 2, naux)), dma((2, 2, naux)),
-        dma((peers,)), dma((peers,)),
-        dma((2,)), dma((2,)),
+        dma((6,)),
+        dma((2, 2)),
+        dma((2, 2)),
+        dma((2, 2)),
+        dma((2,)),
+        dma((6,)),
+        dma((6,)),
     ]
     applied, intersection = pl.pallas_call(
         functools.partial(kernel, naux, ntr),
@@ -358,15 +364,15 @@
             jax.ShapeDtypeStruct((vectors, own_val, cond), F32),
             jax.ShapeDtypeStruct((vectors, vectors), F32),
         ),
-        in_specs=[vmem, vmem, vmem, vmem, hbm, hbm, hbm],
+        in_specs=[pl.BlockSpec(memory_space=pltpu.SMEM)] + [hbm] * 6,
         out_specs=(vmem, vmem),
         scratch_shapes=scratch,
         compiler_params=pltpu.CompilerParams(
-            collective_id=0, has_side_effects=True, vmem_limit_bytes=56 * 1024 * 1024
+            collective_id=0, has_side_effects=True, vmem_limit_bytes=40 * 1024 * 1024
         ),
     )(
-        live_aux.reshape(1, 1), trial_vectors, energy_val.reshape(1, -1),
-        energy_cond.reshape(1, -1), coef_occ, coef_virt, pair_coef,
+        live_aux, *[pltpu.with_memory_space_constraint(x, pltpu.HBM) for x in (
+            trial_vectors, energy_val.reshape(1, -1), energy_cond.reshape(1, -1), coef_occ, coef_virt, pair_coef)]
     )
     return pl.pallas_call(
         finish,
@@ -376,6 +382,7 @@
         ),
         in_specs=[vmem, vmem],
         out_specs=(vmem, vmem),
+        compiler_params=pltpu.CompilerParams(vmem_limit_bytes=2 * 1024 * 1024),
     )(applied, intersection)
 
 

time: 49.1 us -> 45.2 us (0.921)
  Pallas kernels: 47.6 us -> 43.7 us
    pallas_call x1, Pallas kernels: 46.1 us -> 43.1 us  [body(): pl.pallas_call(functools.partial(kernel, naux, ntr), out_shape=(jax.Shape...]
    pallas_call x1, Pallas kernels: 1.5 us -> 0.66 us  [body(): pl.pallas_call(finish, out_shape=(jax.ShapeDtypeStruct(trial_vectors.shap...]
where the time goes in v3:
time: 45.2 us; the launch traced here: 45 us
  Pallas kernels  43.7 us (97%)
  between operations  1.29 us (3%)
    pallas_call x1, Pallas kernels, body(): pl.pallas_call(functools.partial(kernel, naux, ntr), out_shape=(jax.Shape...  43.1 us

profile of v3, /device:TPU:0, one launch (start us, length us, event | category | flops | bytes accessed | tf_op | source)
XLA Modules:
  0.0 45.0 jit_solution(7706132561289519599)
XLA Ops:
  1.3 43.1 %shard_map.86 = (f32[8,8,256]{2,1,0:T(8,128)S(1)}, f32[8,8]{1,0:T(8,128)S(1)}) custom-call(s32[1]{0:T(128)S(6)} %copy.9.live_ref, f32[8,8,256]{2,1,0:T(8,128)} %trial_hbm.1, f32[1,8]{1,0:T(1,128)} %bitcast.3, f32[1,256]{1,0:T(1,128)} %bitcast.2, bf16[64,64,64]{2,1,0:T(8,128)(2,1)} %occ_hbm.1, bf16[64,256,512]{2,1,0:T(8,128)(2,1)} %virt_hbm.1, ...), custom_call_target="tpu_custom_call" | custom-call | tf_op jit(solution)/shard_map/pallas_call | solution.py:361
  44.4 0.7 %shard_map.87 = (f32[8,8,256]{2,1,0:T(8,128)}, f32[8,8]{1,0:T(8,128)}) custom-call(f32[8,8,256]{2,1,0:T(8,128)S(1)} %get-tuple-element.4.applied_ref, f32[8,8]{1,0:T(8,128)S(1)} %get-tuple-element.5.inter_ref), custom_call_target="tpu_custom_call" | custom-call | tf_op jit(solution)/shard_map/pallas_call | solution.py:377

commit v4 on v3

--- a/solution.py
+++ b/solution.py
@@ -10,7 +10,6 @@
 
 F32 = jnp.float32
 BF16 = jnp.bfloat16
-CHUNK = 32
 BLEND = 32
 LANES = 128
 MESH = pl.DeviceIdType.MESH
@@ -34,6 +33,7 @@
     t = lax.axis_index("tr")
     own_val, vectors, cond = trial_ref.shape
     half = vectors // 2
+    size = half // 2
     slots, val, _ = occ.shape
     here = a * ntr + t
 
@@ -44,10 +44,16 @@
     for copy in loads[:3]:
         copy.start()
 
-    everyone = [(da, dt) for da in range(naux) for dt in range(ntr) if (da, dt) != (0, 0)]
+    everyone = [(da, dt) for da in reversed(range(naux)) for dt in reversed(range(ntr)) if (da, dt) != (0, 0)]
+
+    def along(d):
+        if naux & (naux - 1):
+            return lax.rem(a + d, naux)
+        bits = [1 << i for i in range(naux.bit_length()) if d >> i & 1]
+        return a + sum(bit * (1 - 2 * (a // bit % 2)) for bit in bits)
 
     def peer(da, dt):
-        return {"aux": lax.rem(a + da, naux), "tr": lax.rem(t + dt, ntr)}
+        return {"aux": along(da), "tr": lax.rem(t + dt, ntr)}
 
     def send(src, dst, ssem, rsem, device):
         return pltpu.make_async_remote_copy(
@@ -59,9 +65,9 @@
     mate = {"grp": 1 - g}
     barrier = pltpu.get_barrier_semaphore()
     with scope("signals"):
-        for da, dt in everyone:
-            pl.semaphore_signal(barrier, inc=1, device_id=peer(da, dt), device_id_type=MESH)
-        pl.semaphore_signal(barrier, inc=1, device_id=mate, device_id_type=MESH)
+        greeted = [peer(da, 0) for da in reversed(range(1, naux))] + [peer(0, dt) for dt in range(1, ntr)] + [mate]
+        for device in greeted:
+            pl.semaphore_signal(barrier, inc=1, device_id=device, device_id_type=MESH)
     for copy in loads[3:]:
         copy.start()
 
@@ -93,15 +99,6 @@
     def column(row, j):
         return jnp.sum(jnp.where(lane == j * vectors + vector, row, 0.0), axis=1, keepdims=True)
 
-    def contract(cols):
-        acc[...] = jnp.zeros_like(acc)
-
-        @pl.loop(0, slots // CHUNK)
-        def _(i):
-            acc[...] += jnp.dot(
-                blended[i], virt[pl.ds(i * CHUNK, CHUNK), :, cols].reshape(CHUNK * cond, cond),
-                preferred_element_type=F32)
-
     def apply(it, x):
         finals = []
 
@@ -111,17 +108,20 @@
             return copy
 
         with scope("pack"):
-            block = jnp.concatenate(x, axis=1).astype(BF16)
-            block_send[it] = block
-            block_recv[it, a] = block
+            for h in range(2):
+                block = jnp.concatenate(x[h * size:(h + 1) * size], axis=1).astype(BF16)
+                block_send[it, h] = block
+                block_recv[it, h, a] = block
         if it == 0:
             with scope("barrier"):
-                pl.semaphore_wait(barrier, len(everyone) + 1)
+                pl.semaphore_wait(barrier, len(greeted))
         with scope("gather_issue"):
-            for d in range(1, naux):
-                send(block_send.at[it], block_recv.at[it, a], block_sem.at[0, it], block_sem.at[1, it], peer(d, 0)).start()
-            blocks = block_recv.at[it, pl.ds(0, naux - 1)]
-            finals.append(drain(blocks, block_sem.at[0, it]))
+            for h in range(2):
+                for d in reversed(range(1, naux)):
+                    send(block_send.at[it, h], block_recv.at[it, h, a],
+                         block_sem.at[0, it, h], block_sem.at[1, it, h], peer(d, 0)).start()
+                blocks = block_recv.at[it, h, pl.ds(0, naux - 1)]
+                finals.append(drain(blocks, block_sem.at[0, it, h]))
 
         with scope("project"):
             if it == 0:
@@ -150,80 +150,96 @@
                 others = [trial_k[lax.rem(g * half + n, vectors)] for n in range(vectors)]
                 own_row[...] = row_of([[fold(gap * others[j] * others[n]) for n in range(vectors)] for j in range(half)])
 
-        with scope("gather_wait"):
-            drain(blocks, block_sem.at[1, it])()
-        if it == 0:
-            mate_cross = send(cross_recv, mate_recv.at[1], extra_ssem.at[2], extra_rsem.at[2], mate)
-        with scope("proj_issue"):
-            for da, dt in everyone:
-                send(proj_send.at[it], proj_recv.at[it, here], proj_sem.at[0, it], proj_sem.at[1, it], peer(da, dt)).start()
-            projections = proj_recv.at[it, pl.ds(0, len(everyone))]
-            finals.append(drain(projections, proj_sem.at[0, it]))
+        crosses, mates = [], []
+        mate_cross = send(cross_recv, mate_recv.at[1], extra_ssem.at[4], extra_rsem.at[4], mate)
+        for h in range(2):
+            with scope("gather_wait"):
+                drain(block_recv.at[it, h, pl.ds(0, naux - 1)], block_sem.at[1, it, h])()
             if it == 0:
-                mate_own = go(send(block_recv.at[0], mate_recv.at[0], extra_ssem.at[0], extra_rsem.at[0], mate))
-                cross = go(send(block_recv.at[0], cross_recv, extra_ssem.at[1], extra_rsem.at[1], peer(0, 1)))
-        with scope("blend"):
-            wide = jnp.concatenate([block_recv[it, s].astype(F32) for s in range(naux)], axis=0).astype(BF16)
-            columns = [wide[:, k * cond:(k + 1) * cond] for k in range(half)]
-
-            @pl.loop(0, slots // BLEND)
-            def _(i):
-                rows = occ[pl.ds(i * BLEND, BLEND)].reshape(BLEND * val, val)
-                for k in range(half):
-                    b = jnp.dot(rows, columns[k], preferred_element_type=F32).astype(BF16)
-                    for q in range(BLEND):
-                        blended[i * (BLEND // CHUNK) + q // CHUNK, k * val:(k + 1) * val,
-                                (q % CHUNK) * cond:(q % CHUNK + 1) * cond] = b[q * val:(q + 1) * val]
+                crosses.append(go(send(
+                    block_recv.at[0, h], cross_recv.at[h], extra_ssem.at[h], extra_rsem.at[h], peer(0, 1))))
+                mates.append(go(send(
+                    block_recv.at[0, h], mate_recv.at[0, h], extra_ssem.at[2 + h], extra_rsem.at[2 + h], mate)))
+            if h == 1:
+                with scope("proj_issue"):
+                    for da, dt in everyone:
+                        send(proj_send.at[it], proj_recv.at[it, here], proj_sem.at[0, it], proj_sem.at[1, it],
+                             peer(da, dt)).start()
+                    projections = proj_recv.at[it, pl.ds(0, len(everyone))]
+                    finals.append(drain(projections, proj_sem.at[0, it]))
+            with scope("blend"):
+                wide = jnp.concatenate([block_recv[it, h, s].astype(F32) for s in range(naux)], axis=0).astype(BF16)
+                columns = [wide[:, k * cond:(k + 1) * cond] for k in range(size)]
+
+                @pl.loop(0, slots // BLEND)
+                def _(i):
+                    rows = occ[pl.ds(i * BLEND, BLEND)].reshape(BLEND * val, val)
+                    for k in range(size):
+                        b = jnp.dot(rows, columns[k], preferred_element_type=F32).astype(BF16)
+                        for q in range(BLEND):
+                            blended[i, (h * size + k) * val:(h * size + k + 1) * val,
+                                    q * cond:(q + 1) * cond] = b[q * val:(q + 1) * val]
 
         if it == 0:
             with scope("virt_wait"):
                 virt_copy.wait()
 
-        def sum_copies(dt):
-            return [
-                send(sum_send.at[it, dt, lax.rem(a + d, naux)], sum_recv.at[it, dt * naux + d],
-                     sum_sem.at[0, it], sum_sem.at[1, it], peer(d, dt))
-                for d in range(1 - dt, naux)]
-
-        with scope("contract"):
+        def contract(rows, dt):
+            start = pl.multiple_of(lax.rem(t + dt, ntr) * cond, cond)
+            mixture = jnp.concatenate([blended[i, rows, :] for i in range(slots // BLEND)], axis=1)
+            acc[:rows.size] = jnp.dot(
+                mixture, virt[:, :, pl.ds(start, cond)].reshape(slots * cond, cond), preferred_element_type=F32)
+
+        def pack(dt, h, base):
+            for s in range(naux):
+                for k in range(size):
+                    row = base + k * val + s * own_val
+                    sum_send[it, dt, h, s, :, k * cond:(k + 1) * cond] = acc[row:row + own_val, :].astype(BF16)
+
+        def post(dt, h):
+            for d in reversed(range(1 - dt, naux)):
+                send(sum_send.at[it, dt, h, along(d)], sum_recv.at[it, (dt * naux + d) * 2 + h],
+                     sum_sem.at[0, it], sum_sem.at[1, it], peer(d, dt)).start()
+
+        with scope("contract_a"):
+            contract(pl.ds(0, half * val), 1)
+            for h in range(2):
+                pack(1, h, h * size * val)
+                post(1, h)
+        with scope("contract_b"):
             @pl.loop(0, 2)
-            def _(j):
-                start = pl.multiple_of(lax.rem(t + 1 - j, ntr) * cond, cond)
-                contract(pl.ds(start, cond))
-                for s in range(naux):
-                    for k in range(half):
-                        row = k * val + s * own_val
-                        sum_send[it, 1 - j, s, :, k * cond:(k + 1) * cond] = acc[row:row + own_val, :].astype(BF16)
-
-                @pl.when(j == 0)
-                def _():
-                    for copy in sum_copies(1):
-                        copy.start()
-                    if it == 0:
-                        cross.wait_recv()
+            def _(h):
+                contract(pl.ds(pl.multiple_of(h * size * val, size * val), size * val), 0)
+                pack(0, h, 0)
+                post(0, h)
+                if it == 0:
+                    @pl.when(h == 0)
+                    def _():
+                        for copy in crosses:
+                            copy.wait_recv()
                         mate_cross.start()
 
         with scope("sum_issue"):
-            for copy in sum_copies(0):
-                copy.start()
-            sums = sum_recv.at[it, pl.ds(1, len(everyone))]
+            sums = sum_recv.at[it, pl.ds(2, 2 * len(everyone))]
             finals.append(drain(sums, sum_sem.at[0, it]))
             if it == 0:
                 finals.append(mate_cross.wait_send)
 
         if it == 0:
             with scope("overlap"):
-                mate_own.wait_recv()
+                for copy in mates:
+                    copy.wait_recv()
                 mate_cross.wait_recv()
                 parts = [[jnp.zeros((own_val, LANES), F32)] * vectors for _ in range(half)]
                 for dt in range(2):
                     for s in range(naux):
-                        part = sum_send[0, dt, s].astype(F32)
-                        same = (block_recv[0, s] if dt == 0 else cross_recv[s]).astype(F32)
-                        other = mate_recv[dt, s].astype(F32)
-                        both = [y[:, k * cond:(k + 1) * cond] for y in (same, other) for k in range(half)]
+                        same = block_recv.at[0] if dt == 0 else cross_recv
+                        both = [
+                            ref[h, s, :, k * cond:(k + 1) * cond].astype(F32)
+                            for ref in (same, mate_recv.at[dt]) for h in range(2) for k in range(size)]
                         for j in range(half):
-                            mine = part[:, j * cond:(j + 1) * cond]
+                            where = pl.ds(j % size * cond, cond)
+                            mine = sum_send[0, dt, j // size, s, :, where].astype(F32)
                             for n in range(vectors):
                                 parts[j][n] = parts[j][n] + fold(mine * both[n])
                 row = own_row[...] + row_of(parts)
@@ -240,7 +256,7 @@
                 proj += proj_recv[it, n].astype(F32)
             if it == 0:
                 proj_all[...] = proj
-                mate_proj = go(send(proj_all, proj_mate, extra_ssem.at[3], extra_rsem.at[3], mate))
+                mate_proj = go(send(proj_all, proj_mate, extra_ssem.at[5], extra_rsem.at[5], mate))
             proj_b = proj.astype(BF16)
             for v in range(own_val):
                 mixed[v] = lax.dot_general(
@@ -250,10 +266,12 @@
         with scope("sum_wait"):
             drain(sums, sum_sem.at[1, it])()
         with scope("combine"):
-            total = sum_send[it, 0, a].astype(F32)
-            for n in range(1, naux * ntr):
-                total += sum_recv[it, n].astype(F32)
-            result = [local[k] + total[:, k * cond:(k + 1) * cond] for k in range(half)]
+            result = []
+            for h in range(2):
+                total = sum_send[it, 0, h, a].astype(F32)
+                for n in range(1, naux * ntr):
+                    total += sum_recv[it, n * 2 + h].astype(F32)
+                result += [local[h * size + k] + total[:, k * cond:(k + 1) * cond] for k in range(size)]
         return result, proj_b, mate_proj if it == 0 else None, finals
 
     first, proj_b, mate_proj, finals = apply(0, [trial_k[g * half + k] for k in range(half)])
@@ -277,7 +295,7 @@
         for j in range(half):
             square += jnp.where(lane == g * half + j, inter[j], 0.0)
         core_recv[0] = square
-        core_dots = send(core_recv.at[0], core_recv.at[1], extra_ssem.at[4], extra_rsem.at[4], mate)
+        core_dots = send(core_recv.at[0], core_recv.at[1], extra_ssem.at[6], extra_rsem.at[6], mate)
         core_dots.start()
 
         correction = []
@@ -291,7 +309,7 @@
     with scope("final_pack"):
         for k in range(half):
             final_send[k] = second[k]
-        final_copy = send(final_send, final_recv, extra_ssem.at[5], extra_rsem.at[5], mate)
+        final_copy = send(final_send, final_recv, extra_ssem.at[7], extra_rsem.at[7], mate)
         final_copy.start()
         for k in range(half):
             out_ref[g * half + k] = second[k]
@@ -322,7 +340,7 @@
     vmem = pl.BlockSpec(memory_space=pltpu.VMEM)
     hbm = pl.BlockSpec(memory_space=pltpu.HBM)
     dma = pltpu.SemaphoreType.DMA
-    block = (own_val, half * cond)
+    block = (own_val, half // 2 * cond)
     scratch = [
         pltpu.VMEM(trial_vectors.shape, F32),
         pltpu.VMEM((1, own_val), F32),
@@ -330,33 +348,33 @@
         pltpu.VMEM(coef_occ.shape, BF16),
         pltpu.VMEM(coef_virt.shape, BF16),
         pltpu.VMEM(pair_coef.shape, BF16),
-        pltpu.VMEM((slots // CHUNK, half * val, CHUNK * cond), BF16),
+        pltpu.VMEM((slots // BLEND, half * val, BLEND * cond), BF16),
         pltpu.VMEM((half * val, cond), F32),
         pltpu.VMEM((own_val, half, cond), F32),
         pltpu.VMEM((vectors, own_val, cond), F32),
         pltpu.VMEM((1, LANES), F32),
-        pltpu.VMEM((2, *block), BF16),
+        pltpu.VMEM((2, 2, *block), BF16),
+        pltpu.VMEM((2, 2, naux, *block), BF16),
         pltpu.VMEM((2, naux, *block), BF16),
-        pltpu.VMEM((naux, *block), BF16),
-        pltpu.VMEM((2, naux, *block), BF16),
+        pltpu.VMEM((2, 2, naux, *block), BF16),
         pltpu.VMEM((2, half, naux_all), BF16),
         pltpu.VMEM((2, peers, half, naux_all), BF16),
         pltpu.VMEM((half, naux_all), F32),
         pltpu.VMEM((half, naux_all), F32),
-        pltpu.VMEM((2, ntr, naux, *block), BF16),
-        pltpu.VMEM((2, peers, *block), BF16),
+        pltpu.VMEM((2, ntr, 2, naux, *block), BF16),
+        pltpu.VMEM((2, 2 * peers, *block), BF16),
         pltpu.VMEM((1, LANES), F32),
         pltpu.VMEM((peers, 1, LANES), F32),
         pltpu.VMEM((2, vectors, LANES), F32),
         pltpu.VMEM((half, own_val, cond), F32),
         pltpu.VMEM((half, own_val, cond), F32),
         dma((6,)),
-        dma((2, 2)),
+        dma((2, 2, 2)),
         dma((2, 2)),
         dma((2, 2)),
         dma((2,)),
-        dma((6,)),
-        dma((6,)),
+        dma((8,)),
+        dma((8,)),
     ]
     applied, intersection = pl.pallas_call(
         functools.partial(kernel, naux, ntr),
@@ -368,7 +386,7 @@
         out_specs=(vmem, vmem),
         scratch_shapes=scratch,
         compiler_params=pltpu.CompilerParams(
-            collective_id=0, has_side_effects=True, vmem_limit_bytes=40 * 1024 * 1024
+            collective_id=0, has_side_effects=True, vmem_limit_bytes=48 * 1024 * 1024
         ),
     )(
         live_aux, *[pltpu.with_memory_space_constraint(x, pltpu.HBM) for x in (

time: 45.2 us -> 42.9 us (0.949)
  Pallas kernels: 43.7 us -> 41.5 us
    pallas_call x1, Pallas kernels: 43.1 us -> 40.8 us  [body(): pl.pallas_call(functools.partial(kernel, naux, ntr), out_shape=(jax.Shape...]
where the time goes in v4:
time: 42.9 us; the launch traced here: 42.8 us
  Pallas kernels  41.5 us (97%)
  between operations  1.29 us (3%)
    pallas_call x1, Pallas kernels, body(): pl.pallas_call(functools.partial(kernel, naux, ntr), out_shape=(jax.Shape...  40.8 us

profile of v4, /device:TPU:0, one launch (start us, length us, event | category | flops | bytes accessed | tf_op | source)
XLA Modules:
  0.0 42.8 jit_solution(7536045054788387664)
XLA Ops:
  1.3 40.8 %shard_map.86 = (f32[8,8,256]{2,1,0:T(8,128)S(1)}, f32[8,8]{1,0:T(8,128)S(1)}) custom-call(s32[1]{0:T(128)S(6)} %copy.9.live_ref, f32[8,8,256]{2,1,0:T(8,128)} %trial_hbm.1, f32[1,8]{1,0:T(1,128)} %bitcast.3, f32[1,256]{1,0:T(1,128)} %bitcast.2, bf16[64,64,64]{2,1,0:T(8,128)(2,1)} %occ_hbm.1, bf16[64,256,512]{2,1,0:T(8,128)(2,1)} %virt_hbm.1, ...), custom_call_target="tpu_custom_call" | custom-call | tf_op jit(solution)/shard_map/pallas_call | solution.py:379
  42.1 0.7 %shard_map.87 = (f32[8,8,256]{2,1,0:T(8,128)}, f32[8,8]{1,0:T(8,128)}) custom-call(f32[8,8,256]{2,1,0:T(8,128)S(1)} %get-tuple-element.4.applied_ref, f32[8,8]{1,0:T(8,128)S(1)} %get-tuple-element.5.inter_ref), custom_call_target="tpu_custom_call" | custom-call | tf_op jit(solution)/shard_map/pallas_call | solution.py:395

commit v5 on v4

--- a/solution.py
+++ b/solution.py
@@ -10,7 +10,7 @@
 
 F32 = jnp.float32
 BF16 = jnp.bfloat16
-BLEND = 32
+BLEND = 64
 LANES = 128
 MESH = pl.DeviceIdType.MESH
 
@@ -171,8 +171,9 @@
                 wide = jnp.concatenate([block_recv[it, h, s].astype(F32) for s in range(naux)], axis=0).astype(BF16)
                 columns = [wide[:, k * cond:(k + 1) * cond] for k in range(size)]
 
-                @pl.loop(0, slots // BLEND)
-                def _(i):
+                @pl.when(t >= 0)
+                def _():
+                    i = 0
                     rows = occ[pl.ds(i * BLEND, BLEND)].reshape(BLEND * val, val)
                     for k in range(size):
                         b = jnp.dot(rows, columns[k], preferred_element_type=F32).astype(BF16)

time: 42.9 us -> 42.6 us (level)
  no operation moved by 1% of the time
where the time goes in v5:
time: 42.6 us; the launch traced here: 42.4 us
  Pallas kernels  41.2 us (97%)
  between operations  1.29 us (3%)
    pallas_call x1, Pallas kernels, body(): pl.pallas_call(functools.partial(kernel, naux, ntr), out_shape=(jax.Shape...  40.5 us

profile of v5, /device:TPU:0, one launch (start us, length us, event | category | flops | bytes accessed | tf_op | source)
XLA Modules:
  0.0 42.4 jit_solution(13809129306055420701)
XLA Ops:
  1.3 40.5 %shard_map.86 = (f32[8,8,256]{2,1,0:T(8,128)S(1)}, f32[8,8]{1,0:T(8,128)S(1)}) custom-call(s32[1]{0:T(128)S(6)} %copy.9.live_ref, f32[8,8,256]{2,1,0:T(8,128)} %trial_hbm.1, f32[1,8]{1,0:T(1,128)} %bitcast.3, f32[1,256]{1,0:T(1,128)} %bitcast.2, bf16[64,64,64]{2,1,0:T(8,128)(2,1)} %occ_hbm.1, bf16[64,256,512]{2,1,0:T(8,128)(2,1)} %virt_hbm.1, ...), custom_call_target="tpu_custom_call" | custom-call | tf_op jit(solution)/shard_map/pallas_call | solution.py:380
  41.8 0.7 %shard_map.87 = (f32[8,8,256]{2,1,0:T(8,128)}, f32[8,8]{1,0:T(8,128)}) custom-call(f32[8,8,256]{2,1,0:T(8,128)S(1)} %get-tuple-element.4.applied_ref, f32[8,8]{1,0:T(8,128)S(1)} %get-tuple-element.5.inter_ref), custom_call_target="tpu_custom_call" | custom-call | tf_op jit(solution)/shard_map/pallas_call | solution.py:396

commit v6 on v5

--- a/solution.py
+++ b/solution.py
@@ -47,8 +47,7 @@
     everyone = [(da, dt) for da in reversed(range(naux)) for dt in reversed(range(ntr)) if (da, dt) != (0, 0)]
 
     def along(d):
-        if naux & (naux - 1):
-            return lax.rem(a + d, naux)
+        assert naux & (naux - 1) == 0
         bits = [1 << i for i in range(naux.bit_length()) if d >> i & 1]
         return a + sum(bit * (1 - 2 * (a // bit % 2)) for bit in bits)
 
@@ -185,43 +184,53 @@
             with scope("virt_wait"):
                 virt_copy.wait()
 
+        part = val // 2
+        owners = naux // 2
+
         def contract(rows, dt):
             start = pl.multiple_of(lax.rem(t + dt, ntr) * cond, cond)
-            mixture = jnp.concatenate([blended[i, rows, :] for i in range(slots // BLEND)], axis=1)
-            acc[:rows.size] = jnp.dot(
+            mixture = jnp.concatenate([
+                jnp.concatenate([blended[i, ds, :] for i in range(slots // BLEND)], axis=1) for ds in rows], axis=0)
+            acc[:mixture.shape[0]] = jnp.dot(
                 mixture, virt[:, :, pl.ds(start, cond)].reshape(slots * cond, cond), preferred_element_type=F32)
 
-        def pack(dt, h, base):
+        def pack(dt, s, rows):
+            for k in range(half):
+                sum_send[it, dt, s, :, k * cond:(k + 1) * cond] = acc[pl.ds(rows[k], own_val), :].astype(BF16)
+
+        def post(dt, partners):
+            for d in reversed(partners):
+                send(sum_send.at[it, dt, along(d)], sum_recv.at[it, dt * naux + d],
+                     sum_sem.at[0, it], sum_sem.at[1, it], peer(d, dt)).start()
+
+        with scope("contract_a"):
+            contract([pl.ds(0, half * val)], 1)
             for s in range(naux):
-                for k in range(size):
-                    row = base + k * val + s * own_val
-                    sum_send[it, dt, h, s, :, k * cond:(k + 1) * cond] = acc[row:row + own_val, :].astype(BF16)
-
-        def post(dt, h):
-            for d in reversed(range(1 - dt, naux)):
-                send(sum_send.at[it, dt, h, along(d)], sum_recv.at[it, (dt * naux + d) * 2 + h],
-                     sum_sem.at[0, it], sum_sem.at[1, it], peer(d, dt)).start()
-
-        with scope("contract_a"):
-            contract(pl.ds(0, half * val), 1)
-            for h in range(2):
-                pack(1, h, h * size * val)
-                post(1, h)
+                pack(1, s, [k * val + s * own_val for k in range(half)])
+            post(1, range(naux))
         with scope("contract_b"):
             @pl.loop(0, 2)
             def _(h):
-                contract(pl.ds(pl.multiple_of(h * size * val, size * val), size * val), 0)
-                pack(0, h, 0)
-                post(0, h)
-                if it == 0:
-                    @pl.when(h == 0)
-                    def _():
+                side = lax.rem(a // owners + 1 + h, 2)
+                contract([
+                    pl.ds(pl.multiple_of(k * val + side * part, part), part) for k in range(half)], 0)
+                for s in range(owners):
+                    pack(0, side * owners + s, [k * part + s * own_val for k in range(half)])
+
+                @pl.when(h == 0)
+                def _():
+                    post(0, range(owners, naux))
+                    if it == 0:
                         for copy in crosses:
                             copy.wait_recv()
                         mate_cross.start()
 
+                @pl.when(h == 1)
+                def _():
+                    post(0, range(1, owners))
+
         with scope("sum_issue"):
-            sums = sum_recv.at[it, pl.ds(2, 2 * len(everyone))]
+            sums = sum_recv.at[it, pl.ds(1, len(everyone))]
             finals.append(drain(sums, sum_sem.at[0, it]))
             if it == 0:
                 finals.append(mate_cross.wait_send)
@@ -239,8 +248,7 @@
                             ref[h, s, :, k * cond:(k + 1) * cond].astype(F32)
                             for ref in (same, mate_recv.at[dt]) for h in range(2) for k in range(size)]
                         for j in range(half):
-                            where = pl.ds(j % size * cond, cond)
-                            mine = sum_send[0, dt, j // size, s, :, where].astype(F32)
+                            mine = sum_send[0, dt, s, :, j * cond:(j + 1) * cond].astype(F32)
                             for n in range(vectors):
                                 parts[j][n] = parts[j][n] + fold(mine * both[n])
                 row = own_row[...] + row_of(parts)
@@ -267,12 +275,10 @@
         with scope("sum_wait"):
             drain(sums, sum_sem.at[1, it])()
         with scope("combine"):
-            result = []
-            for h in range(2):
-                total = sum_send[it, 0, h, a].astype(F32)
-                for n in range(1, naux * ntr):
-                    total += sum_recv[it, n * 2 + h].astype(F32)
-                result += [local[h * size + k] + total[:, k * cond:(k + 1) * cond] for k in range(size)]
+            total = sum_send[it, 0, a].astype(F32)
+            for n in range(1, naux * ntr):
+                total += sum_recv[it, n].astype(F32)
+            result = [local[k] + total[:, k * cond:(k + 1) * cond] for k in range(half)]
         return result, proj_b, mate_proj if it == 0 else None, finals
 
     first, proj_b, mate_proj, finals = apply(0, [trial_k[g * half + k] for k in range(half)])
@@ -362,8 +368,8 @@
         pltpu.VMEM((2, peers, half, naux_all), BF16),
         pltpu.VMEM((half, naux_all), F32),
         pltpu.VMEM((half, naux_all), F32),
-        pltpu.VMEM((2, ntr, 2, naux, *block), BF16),
-        pltpu.VMEM((2, 2 * peers, *block), BF16),
+        pltpu.VMEM((2, ntr, naux, own_val, half * cond), BF16),
+        pltpu.VMEM((2, peers, own_val, half * cond), BF16),
         pltpu.VMEM((1, LANES), F32),
         pltpu.VMEM((peers, 1, LANES), F32),
         pltpu.VMEM((2, vectors, LANES), F32),

time: 42.6 us -> 42 us (0.986)
  Pallas kernels: 41.2 us -> 40.5 us
    pallas_call x1, Pallas kernels: 40.5 us -> 39.9 us  [body(): pl.pallas_call(functools.partial(kernel, naux, ntr), out_shape=(jax.Shape...]
where the time goes in v6:
time: 42 us; the launch traced here: 41.8 us
  Pallas kernels  40.5 us (96%)
  between operations  1.29 us (3%)
    pallas_call x1, Pallas kernels, body(): pl.pallas_call(functools.partial(kernel, naux, ntr), out_shape=(jax.Shape...  39.9 us

profile of v6, /device:TPU:0, one launch (start us, length us, event | category | flops | bytes accessed | tf_op | source)
XLA Modules:
  0.0 41.8 jit_solution(16857960966315514154)
XLA Ops:
  1.3 39.9 %shard_map.86 = (f32[8,8,256]{2,1,0:T(8,128)S(1)}, f32[8,8]{1,0:T(8,128)S(1)}) custom-call(s32[1]{0:T(128)S(6)} %copy.9.live_ref, f32[8,8,256]{2,1,0:T(8,128)} %trial_hbm.1, f32[1,8]{1,0:T(1,128)} %bitcast.3, f32[1,256]{1,0:T(1,128)} %bitcast.2, bf16[64,64,64]{2,1,0:T(8,128)(2,1)} %occ_hbm.1, bf16[64,256,512]{2,1,0:T(8,128)(2,1)} %virt_hbm.1, ...), custom_call_target="tpu_custom_call" | custom-call | tf_op jit(solution)/shard_map/pallas_call | solution.py:386
  41.1 0.7 %shard_map.87 = (f32[8,8,256]{2,1,0:T(8,128)}, f32[8,8]{1,0:T(8,128)}) custom-call(f32[8,8,256]{2,1,0:T(8,128)S(1)} %get-tuple-element.4.applied_ref, f32[8,8]{1,0:T(8,128)S(1)} %get-tuple-element.5.inter_ref), custom_call_target="tpu_custom_call" | custom-call | tf_op jit(solution)/shard_map/pallas_call | solution.py:402

commit v7 on v6

--- a/solution.py
+++ b/solution.py
@@ -38,9 +38,11 @@
     here = a * ntr + t
 
     arrays = ((trial_hbm, trial_ref), (val_hbm, val_ref), (cond_hbm, cond_ref),
-              (pair_hbm, pair), (occ_hbm, occ), (virt_hbm, virt))
+              (pair_hbm, pair), (occ_hbm, occ)) + tuple(
+        (virt_hbm.at[:, :, pl.ds(pl.multiple_of(lax.rem(t + dt, ntr) * cond, cond), cond)], virt.at[dt])
+        for dt in (1, 0))
     loads = [pltpu.make_async_copy(src, dst, load_sem.at[n]) for n, (src, dst) in enumerate(arrays)]
-    pair_copy, occ_copy, virt_copy = loads[3:]
+    pair_copy, occ_copy, *virt_copies = loads[3:]
     for copy in loads[:3]:
         copy.start()
 
@@ -170,7 +172,7 @@
                 wide = jnp.concatenate([block_recv[it, h, s].astype(F32) for s in range(naux)], axis=0).astype(BF16)
                 columns = [wide[:, k * cond:(k + 1) * cond] for k in range(size)]
 
-                @pl.when(t >= 0)
+                @pl.when((t, a)[h] >= 0)
                 def _():
                     i = 0
                     rows = occ[pl.ds(i * BLEND, BLEND)].reshape(BLEND * val, val)
@@ -182,17 +184,17 @@
 
         if it == 0:
             with scope("virt_wait"):
-                virt_copy.wait()
+                for copy in virt_copies:
+                    copy.wait()
 
         part = val // 2
         owners = naux // 2
 
         def contract(rows, dt):
-            start = pl.multiple_of(lax.rem(t + dt, ntr) * cond, cond)
             mixture = jnp.concatenate([
                 jnp.concatenate([blended[i, ds, :] for i in range(slots // BLEND)], axis=1) for ds in rows], axis=0)
             acc[:mixture.shape[0]] = jnp.dot(
-                mixture, virt[:, :, pl.ds(start, cond)].reshape(slots * cond, cond), preferred_element_type=F32)
+                mixture, virt[dt].reshape(slots * cond, cond), preferred_element_type=F32)
 
         def pack(dt, s, rows):
             for k in range(half):
@@ -204,10 +206,12 @@
                      sum_sem.at[0, it], sum_sem.at[1, it], peer(d, dt)).start()
 
         with scope("contract_a"):
-            contract([pl.ds(0, half * val)], 1)
-            for s in range(naux):
-                pack(1, s, [k * val + s * own_val for k in range(half)])
-            post(1, range(naux))
+            @pl.when(g >= 0)
+            def _():
+                contract([pl.ds(0, half * val)], 1)
+                for s in range(naux):
+                    pack(1, s, [k * val + s * own_val for k in range(half)])
+                post(1, range(naux))
         with scope("contract_b"):
             @pl.loop(0, 2)
             def _(h):
@@ -353,7 +357,7 @@
         pltpu.VMEM((1, own_val), F32),
         pltpu.VMEM((1, cond), F32),
         pltpu.VMEM(coef_occ.shape, BF16),
-        pltpu.VMEM(coef_virt.shape, BF16),
+        pltpu.VMEM((ntr, slots, cond, cond), BF16),
         pltpu.VMEM(pair_coef.shape, BF16),
         pltpu.VMEM((slots // BLEND, half * val, BLEND * cond), BF16),
         pltpu.VMEM((half * val, cond), F32),
@@ -375,7 +379,7 @@
         pltpu.VMEM((2, vectors, LANES), F32),
         pltpu.VMEM((half, own_val, cond), F32),
         pltpu.VMEM((half, own_val, cond), F32),
-        dma((6,)),
+        dma((7,)),
         dma((2, 2, 2)),
         dma((2, 2)),
         dma((2, 2)),

time: 42 us -> 41.5 us (0.988)
  Pallas kernels: 40.5 us -> 40 us
    pallas_call x1, Pallas kernels: 39.9 us -> 39.4 us  [body(): pl.pallas_call(functools.partial(kernel, naux, ntr), out_shape=(jax.Shape...]
where the time goes in v7:
time: 41.5 us; the launch traced here: 41.3 us
  Pallas kernels  40 us (96%)
  between operations  1.29 us (3%)
    pallas_call x1, Pallas kernels, body(): pl.pallas_call(functools.partial(kernel, naux, ntr), out_shape=(jax.Shape...  39.4 us

profile of v7, /device:TPU:0, one launch (start us, length us, event | category | flops | bytes accessed | tf_op | source)
XLA Modules:
  0.0 41.3 jit_solution(9520641945982292822)
XLA Ops:
  1.3 39.4 %shard_map.86 = (f32[8,8,256]{2,1,0:T(8,128)S(1)}, f32[8,8]{1,0:T(8,128)S(1)}) custom-call(s32[1]{0:T(128)S(6)} %copy.9.live_ref, f32[8,8,256]{2,1,0:T(8,128)} %trial_hbm.1, f32[1,8]{1,0:T(1,128)} %bitcast.3, f32[1,256]{1,0:T(1,128)} %bitcast.2, bf16[64,64,64]{2,1,0:T(8,128)(2,1)} %occ_hbm.1, bf16[64,256,512]{2,1,0:T(8,128)(2,1)} %virt_hbm.1, ...), custom_call_target="tpu_custom_call" | custom-call | tf_op jit(solution)/shard_map/pallas_call | solution.py:390
  40.7 0.7 %shard_map.87 = (f32[8,8,256]{2,1,0:T(8,128)}, f32[8,8]{1,0:T(8,128)}) custom-call(f32[8,8,256]{2,1,0:T(8,128)S(1)} %get-tuple-element.4.applied_ref, f32[8,8]{1,0:T(8,128)S(1)} %get-tuple-element.5.inter_ref), custom_call_target="tpu_custom_call" | custom-call | tf_op jit(solution)/shard_map/pallas_call | solution.py:406

commit v8 on v7

--- a/solution.py
+++ b/solution.py
@@ -212,26 +212,34 @@
                 for s in range(naux):
                     pack(1, s, [k * val + s * own_val for k in range(half)])
                 post(1, range(naux))
-        with scope("contract_b"):
-            @pl.loop(0, 2)
-            def _(h):
-                side = lax.rem(a // owners + 1 + h, 2)
-                contract([
-                    pl.ds(pl.multiple_of(k * val + side * part, part), part) for k in range(half)], 0)
-                for s in range(owners):
-                    pack(0, side * owners + s, [k * part + s * own_val for k in range(half)])
-
-                @pl.when(h == 0)
+        if it == 0:
+            with scope("cross_wait"):
+                for copy in crosses:
+                    copy.wait_recv()
+                mate_cross.start()
+            with scope("contract_b"):
+                @pl.when(t >= 0)
                 def _():
-                    post(0, range(owners, naux))
-                    if it == 0:
-                        for copy in crosses:
-                            copy.wait_recv()
-                        mate_cross.start()
-
-                @pl.when(h == 1)
-                def _():
-                    post(0, range(1, owners))
+                    contract([pl.ds(0, half * val)], 0)
+                    for s in range(naux):
+                        pack(0, s, [k * val + s * own_val for k in range(half)])
+        else:
+            with scope("contract_b"):
+                @pl.loop(0, 2)
+                def _(h):
+                    side = lax.rem(a // owners + 1 + h, 2)
+                    contract([
+                        pl.ds(pl.multiple_of(k * val + side * part, part), part) for k in range(half)], 0)
+                    for s in range(owners):
+                        pack(0, side * owners + s, [k * part + s * own_val for k in range(half)])
+
+                    @pl.when(h == 0)
+                    def _():
+                        post(0, range(owners, naux))
+
+                    @pl.when(h == 1)
+                    def _():
+                        post(0, range(1, owners))
 
         with scope("sum_issue"):
             sums = sum_recv.at[it, pl.ds(1, len(everyone))]
@@ -261,6 +269,7 @@
             with scope("dots_issue"):
                 for da, dt in everyone:
                     send(dots_send, dots_recv.at[here], dots_sem.at[0], dots_sem.at[1], peer(da, dt)).start()
+                post(0, range(1, naux))
 
         with scope("exchange"):
             drain(projections, proj_sem.at[1, it])()

time: 41.5 us -> 41 us (0.988)
    pallas_call x1, Pallas kernels: 39.4 us -> 38.9 us  [body(): pl.pallas_call(functools.partial(kernel, naux, ntr), out_shape=(jax.Shape...]
where the time goes in v8:
time: 41 us; the launch traced here: 40.9 us
  Pallas kernels  39.6 us (97%)
  between operations  1.29 us (3%)
    pallas_call x1, Pallas kernels, body(): pl.pallas_call(functools.partial(kernel, naux, ntr), out_shape=(jax.Shape...  38.9 us

profile of v8, /device:TPU:0, one launch (start us, length us, event | category | flops | bytes accessed | tf_op | source)
XLA Modules:
  0.0 40.9 jit_solution(16156877017584526624)
XLA Ops:
  1.3 38.9 %shard_map.86 = (f32[8,8,256]{2,1,0:T(8,128)S(1)}, f32[8,8]{1,0:T(8,128)S(1)}) custom-call(s32[1]{0:T(128)S(6)} %copy.9.live_ref, f32[8,8,256]{2,1,0:T(8,128)} %trial_hbm.1, f32[1,8]{1,0:T(1,128)} %bitcast.3, f32[1,256]{1,0:T(1,128)} %bitcast.2, bf16[64,64,64]{2,1,0:T(8,128)(2,1)} %occ_hbm.1, bf16[64,256,512]{2,1,0:T(8,128)(2,1)} %virt_hbm.1, ...), custom_call_target="tpu_custom_call" | custom-call | tf_op jit(solution)/shard_map/pallas_call | solution.py:399
  40.2 0.7 %shard_map.87 = (f32[8,8,256]{2,1,0:T(8,128)}, f32[8,8]{1,0:T(8,128)}) custom-call(f32[8,8,256]{2,1,0:T(8,128)S(1)} %get-tuple-element.4.applied_ref, f32[8,8]{1,0:T(8,128)S(1)} %get-tuple-element.5.inter_ref), custom_call_target="tpu_custom_call" | custom-call | tf_op jit(solution)/shard_map/pallas_call | solution.py:415

commit v9 on v8

--- a/solution.py
+++ b/solution.py
@@ -48,13 +48,15 @@
 
     everyone = [(da, dt) for da in reversed(range(naux)) for dt in reversed(range(ntr)) if (da, dt) != (0, 0)]
 
-    def along(d):
-        assert naux & (naux - 1) == 0
-        bits = [1 << i for i in range(naux.bit_length()) if d >> i & 1]
-        return a + sum(bit * (1 - 2 * (a // bit % 2)) for bit in bits)
+    assert naux & (naux - 1) == 0
+    partners = [a]
+    for bit in [1 << i for i in range(naux.bit_length() - 1)]:
+        step = bit * (1 - 2 * lax.rem(lax.div(a, bit), 2))
+        partners += [p + step for p in partners]
+    others = [t] + [lax.rem(t + dt, ntr) for dt in range(1, ntr)]
 
     def peer(da, dt):
-        return {"aux": along(da), "tr": lax.rem(t + dt, ntr)}
+        return {"aux": partners[da], "tr": others[dt]}
 
     def send(src, dst, ssem, rsem, device):
         return pltpu.make_async_remote_copy(
@@ -100,7 +102,7 @@
     def column(row, j):
         return jnp.sum(jnp.where(lane == j * vectors + vector, row, 0.0), axis=1, keepdims=True)
 
-    def apply(it, x):
+    def apply(it, vectors_of):
         finals = []
 
         def go(copy):
@@ -108,16 +110,16 @@
             finals.append(copy.wait_send)
             return copy
 
-        with scope("pack"):
+        if it == 0:
+            with scope("barrier"):
+                pl.semaphore_wait(barrier, len(greeted))
+        x = []
+        with scope("gather_issue"):
             for h in range(2):
-                block = jnp.concatenate(x[h * size:(h + 1) * size], axis=1).astype(BF16)
+                x += vectors_of(h)
+                block = jnp.concatenate(x[h * size:], axis=1).astype(BF16)
                 block_send[it, h] = block
                 block_recv[it, h, a] = block
-        if it == 0:
-            with scope("barrier"):
-                pl.semaphore_wait(barrier, len(greeted))
-        with scope("gather_issue"):
-            for h in range(2):
                 for d in reversed(range(1, naux)):
                     send(block_send.at[it, h], block_recv.at[it, h, a],
                          block_sem.at[0, it, h], block_sem.at[1, it, h], peer(d, 0)).start()
@@ -148,8 +150,8 @@
                         keep = jnp.full((val, val), jnp.where(p < live, 1.0, 0.0), F32).astype(BF16)
                         occ[p] = occ[p] * keep
 
-                others = [trial_k[lax.rem(g * half + n, vectors)] for n in range(vectors)]
-                own_row[...] = row_of([[fold(gap * others[j] * others[n]) for n in range(vectors)] for j in range(half)])
+                trials = [trial_k[lax.rem(g * half + n, vectors)] for n in range(vectors)]
+                own_row[...] = row_of([[fold(gap * trials[j] * trials[n]) for n in range(vectors)] for j in range(half)])
 
         crosses, mates = [], []
         mate_cross = send(cross_recv, mate_recv.at[1], extra_ssem.at[4], extra_rsem.at[4], mate)
@@ -200,9 +202,9 @@
             for k in range(half):
                 sum_send[it, dt, s, :, k * cond:(k + 1) * cond] = acc[pl.ds(rows[k], own_val), :].astype(BF16)
 
-        def post(dt, partners):
-            for d in reversed(partners):
-                send(sum_send.at[it, dt, along(d)], sum_recv.at[it, dt * naux + d],
+        def post(dt, steps):
+            for d in reversed(steps):
+                send(sum_send.at[it, dt, partners[d]], sum_recv.at[it, dt * naux + d],
                      sum_sem.at[0, it], sum_sem.at[1, it], peer(d, dt)).start()
 
         with scope("contract_a"):
@@ -285,6 +287,14 @@
                     proj_b, pair[v], (((1,), (1,)), ((), ())), preferred_element_type=F32)
             local = [gap * x[k] + mixed[:, k, :] for k in range(half)]
 
+        exchanged = []
+        if it == 0:
+            mate_proj.wait_recv()
+            both = jnp.concatenate([proj_all[...], proj_mate[...]], axis=0)
+            both = jnp.where(g == 0, both, jnp.concatenate([proj_mate[...], proj_all[...]], axis=0))
+            exchanged = [
+                jnp.sum(fold(both * proj_b[j:j + 1].astype(F32)), axis=1, keepdims=True) for j in range(half)]
+
         with scope("sum_wait"):
             drain(sums, sum_sem.at[1, it])()
         with scope("combine"):
@@ -292,12 +302,11 @@
             for n in range(1, naux * ntr):
                 total += sum_recv[it, n].astype(F32)
             result = [local[k] + total[:, k * cond:(k + 1) * cond] for k in range(half)]
-        return result, proj_b, mate_proj if it == 0 else None, finals
-
-    first, proj_b, mate_proj, finals = apply(0, [trial_k[g * half + k] for k in range(half)])
+        return result, exchanged, finals
+
+    first, exchanged, finals = apply(0, lambda h: [trial_k[g * half + h * size + k] for k in range(size)])
 
     with scope("dots_wait"):
-        mate_proj.wait_recv()
         dots = dots_recv.at[pl.ds(0, len(everyone))]
         drain(dots, dots_sem.at[1])()
         finals.append(drain(dots, dots_sem.at[0]))
@@ -305,27 +314,26 @@
         row = dots_recv[0]
         for n in range(1, naux * ntr):
             row += dots_recv[n]
-        both = jnp.concatenate([proj_all[...], proj_mate[...]], axis=0)
-        both = jnp.where(g == 0, both, jnp.concatenate([proj_mate[...], proj_all[...]], axis=0))
         inter = []
         for j in range(half):
-            exchanged = jnp.sum(fold(both * proj_b[j:j + 1].astype(F32)), axis=1, keepdims=True)
-            inter.append((column(row, j) + exchanged) / (naux * own_val * ntr * cond))
+            inter.append((column(row, j) + exchanged[j]) / (naux * own_val * ntr * cond))
+    def correction(h):
+        corrected = []
+        for j in range(h * size, (h + 1) * size):
+            fitted = trial_k[0] * inter[j][0:1, :]
+            for k in range(1, vectors):
+                fitted += trial_k[k] * inter[j][k:k + 1, :]
+            corrected.append((first[j] - fitted) / gap)
+        return corrected
+
+    second, _, more = apply(1, correction)
+    with scope("core_dots"):
         square = jnp.zeros((vectors, LANES), F32)
         for j in range(half):
             square += jnp.where(lane == g * half + j, inter[j], 0.0)
         core_recv[0] = square
         core_dots = send(core_recv.at[0], core_recv.at[1], extra_ssem.at[6], extra_rsem.at[6], mate)
         core_dots.start()
-
-        correction = []
-        for j in range(half):
-            fitted = trial_k[0] * inter[j][0:1, :]
-            for k in range(1, vectors):
-                fitted += trial_k[k] * inter[j][k:k + 1, :]
-            correction.append((first[j] - fitted) / gap)
-
-    second, _, _, more = apply(1, correction)
     with scope("final_pack"):
         for k in range(half):
             final_send[k] = second[k]

time: 41 us -> 41 us (level)
  no operation moved by 1% of the time
where the time goes in v9:
time: 41 us; the launch traced here: 40.8 us
  Pallas kernels  39.6 us (97%)
  between operations  1.29 us (3%)
    pallas_call x1, Pallas kernels, body(): pl.pallas_call(functools.partial(kernel, naux, ntr), out_shape=(jax.Shape...  38.9 us

profile of v9, /device:TPU:0, one launch (start us, length us, event | category | flops | bytes accessed | tf_op | source)
XLA Modules:
  0.0 40.8 jit_solution(4779581246811016059)
XLA Ops:
  1.3 38.9 %shard_map.86 = (f32[8,8,256]{2,1,0:T(8,128)S(1)}, f32[8,8]{1,0:T(8,128)S(1)}) custom-call(s32[1]{0:T(128)S(6)} %copy.9.live_ref, f32[8,8,256]{2,1,0:T(8,128)} %trial_hbm.1, f32[1,8]{1,0:T(1,128)} %bitcast.3, f32[1,256]{1,0:T(1,128)} %bitcast.2, bf16[64,64,64]{2,1,0:T(8,128)(2,1)} %occ_hbm.1, bf16[64,256,512]{2,1,0:T(8,128)(2,1)} %virt_hbm.1, ...), custom_call_target="tpu_custom_call" | custom-call | tf_op jit(solution)/shard_map/pallas_call | solution.py:407
  40.2 0.7 %shard_map.87 = (f32[8,8,256]{2,1,0:T(8,128)}, f32[8,8]{1,0:T(8,128)}) custom-call(f32[8,8,256]{2,1,0:T(8,128)S(1)} %get-tuple-element.4.applied_ref, f32[8,8]{1,0:T(8,128)S(1)} %get-tuple-element.5.inter_ref), custom_call_target="tpu_custom_call" | custom-call | tf_op jit(solution)/shard_map/pallas_call | solution.py:423

commit v10 on v9

--- a/solution.py
+++ b/solution.py
@@ -153,16 +153,13 @@
                 trials = [trial_k[lax.rem(g * half + n, vectors)] for n in range(vectors)]
                 own_row[...] = row_of([[fold(gap * trials[j] * trials[n]) for n in range(vectors)] for j in range(half)])
 
-        crosses, mates = [], []
-        mate_cross = send(cross_recv, mate_recv.at[1], extra_ssem.at[4], extra_rsem.at[4], mate)
+        mate_cross = send(cross_recv, mate_recv.at[1], extra_ssem.at[2], extra_rsem.at[2], mate)
         for h in range(2):
             with scope("gather_wait"):
                 drain(block_recv.at[it, h, pl.ds(0, naux - 1)], block_sem.at[1, it, h])()
             if it == 0:
-                crosses.append(go(send(
-                    block_recv.at[0, h], cross_recv.at[h], extra_ssem.at[h], extra_rsem.at[h], peer(0, 1))))
-                mates.append(go(send(
-                    block_recv.at[0, h], mate_recv.at[0, h], extra_ssem.at[2 + h], extra_rsem.at[2 + h], mate)))
+                send(block_recv.at[0, h], cross_recv.at[h], extra_ssem.at[0], extra_rsem.at[0], peer(0, 1)).start()
+                send(block_recv.at[0, h], mate_recv.at[0, h], extra_ssem.at[1], extra_rsem.at[1], mate).start()
             if h == 1:
                 with scope("proj_issue"):
                     for da, dt in everyone:
@@ -216,8 +213,8 @@
                 post(1, range(naux))
         if it == 0:
             with scope("cross_wait"):
-                for copy in crosses:
-                    copy.wait_recv()
+                drain(cross_recv, extra_rsem.at[0])()
+                finals.append(drain(cross_recv, extra_ssem.at[0]))
                 mate_cross.start()
             with scope("contract_b"):
                 @pl.when(t >= 0)
@@ -251,8 +248,8 @@
 
         if it == 0:
             with scope("overlap"):
-                for copy in mates:
-                    copy.wait_recv()
+                drain(mate_recv.at[0], extra_rsem.at[1])()
+                finals.append(drain(mate_recv.at[0], extra_ssem.at[1]))
                 mate_cross.wait_recv()
                 parts = [[jnp.zeros((own_val, LANES), F32)] * vectors for _ in range(half)]
                 for dt in range(2):
@@ -280,7 +277,7 @@
                 proj += proj_recv[it, n].astype(F32)
             if it == 0:
                 proj_all[...] = proj
-                mate_proj = go(send(proj_all, proj_mate, extra_ssem.at[5], extra_rsem.at[5], mate))
+                mate_proj = go(send(proj_all, proj_mate, extra_ssem.at[3], extra_rsem.at[3], mate))
             proj_b = proj.astype(BF16)
             for v in range(own_val):
                 mixed[v] = lax.dot_general(
@@ -332,12 +329,12 @@
         for j in range(half):
             square += jnp.where(lane == g * half + j, inter[j], 0.0)
         core_recv[0] = square
-        core_dots = send(core_recv.at[0], core_recv.at[1], extra_ssem.at[6], extra_rsem.at[6], mate)
+        core_dots = send(core_recv.at[0], core_recv.at[1], extra_ssem.at[4], extra_rsem.at[4], mate)
         core_dots.start()
     with scope("final_pack"):
         for k in range(half):
             final_send[k] = second[k]
-        final_copy = send(final_send, final_recv, extra_ssem.at[7], extra_rsem.at[7], mate)
+        final_copy = send(final_send, final_recv, extra_ssem.at[5], extra_rsem.at[5], mate)
         final_copy.start()
         for k in range(half):
             out_ref[g * half + k] = second[k]
@@ -401,8 +398,8 @@
         dma((2, 2)),
         dma((2, 2)),
         dma((2,)),
-        dma((8,)),
-        dma((8,)),
+        dma((6,)),
+        dma((6,)),
     ]
     applied, intersection = pl.pallas_call(
         functools.partial(kernel, naux, ntr),

time: 41 us -> 41 us (level)
  no operation moved by 1% of the time
where the time goes in v10:
time: 41 us; the launch traced here: 40.8 us
  Pallas kernels  39.5 us (96%)
  between operations  1.29 us (3%)
    pallas_call x1, Pallas kernels, body(): pl.pallas_call(functools.partial(kernel, naux, ntr), out_shape=(jax.Shape...  38.9 us

profile of v10, /device:TPU:0, one launch (start us, length us, event | category | flops | bytes accessed | tf_op | source)
XLA Modules:
  0.0 40.8 jit_solution(143389424538684014)
XLA Ops:
  1.3 38.9 %shard_map.86 = (f32[8,8,256]{2,1,0:T(8,128)S(1)}, f32[8,8]{1,0:T(8,128)S(1)}) custom-call(s32[1]{0:T(128)S(6)} %copy.9.live_ref, f32[8,8,256]{2,1,0:T(8,128)} %trial_hbm.1, f32[1,8]{1,0:T(1,128)} %bitcast.3, f32[1,256]{1,0:T(1,128)} %bitcast.2, bf16[64,64,64]{2,1,0:T(8,128)(2,1)} %occ_hbm.1, bf16[64,256,512]{2,1,0:T(8,128)(2,1)} %virt_hbm.1, ...), custom_call_target="tpu_custom_call" | custom-call | tf_op jit(solution)/shard_map/pallas_call | solution.py:404
  40.1 0.7 %shard_map.87 = (f32[8,8,256]{2,1,0:T(8,128)}, f32[8,8]{1,0:T(8,128)}) custom-call(f32[8,8,256]{2,1,0:T(8,128)S(1)} %get-tuple-element.4.applied_ref, f32[8,8]{1,0:T(8,128)S(1)} %get-tuple-element.5.inter_ref), custom_call_target="tpu_custom_call" | custom-call | tf_op jit(solution)/shard_map/pallas_call | solution.py:420
